TPU v7x, 128 devices: a whole 4x4x4 slice. The times are simulated.
128 devices in a mesh: tiles: 32 (over z, x, core), ens: 4 (over y).
Axes of the slice: x: 4, y: 4, z: 4, core: 2. Of those that a mesh axis runs over, the one named last changes fastest.
Arguments:
- depth: float32 [8, 512, 16384], P('ens', 'tiles'), may hold values from 0.3 to 1.5
- bed: float32 [512, 16384], P('tiles'), may hold values from -1.5 to 1.5
- rain: float32 [8, 512, 16384], P('ens', 'tiles'), may hold values from 0.005 to 0.05
- rough_class: int32 [512, 16384], P('tiles'), may hold values from 0 to 15
- class_n: float32 [16], replicated, may hold values from 0.5 to 2
- contact_seg: int32 [32, 32, 8], P('tiles'), may hold values from 0 to 1023, as said below
- contact_lake: int32 [32, 32, 8], P('tiles'), may hold values from -1 to 1279, as said below
- lake_slot: int32 [1280], replicated, may hold values from 0 to 1279, as said below
- storage: float32 [8, 1280], P('ens', 'tiles'), may hold values from 0.5 to 3
- area: float32 [1280], P('tiles'), may hold values from 1 to 4
- release: float32 [1280], P('tiles'), may hold values from 0.5 to 0.98
- upstream_link: int32 [1280], P('tiles'), may hold values from 0 to 1, as said below
Outputs:
- new_depth: float32 [8, 512, 16384], P('ens', 'tiles')
- new_storage: float32 [8, 1280], P('ens', 'tiles')
- ens_outflow: float32 [1280], P('tiles')
Inputs may be any that keep to these rules, and one draw needn't show every extreme that they name: `contact_seg`: within one source tile the segments of all contact slots are distinct. `contact_lake`: A live entry [d, e, c] names a lake whose slot lake_slot lies on owner tile e (slots e * 40 onward); at most 8 live contacts go from one tile to one owner, and some owner receives 8 from every tile. `lake_slot`: A permutation of the slots. `upstream_link`: slots with index below 40 have 0; runs of linked slots form cascades of at most 16 reservoirs, and one cascade has exactly 16.
All inputs are finite; a program needn't handle non-finite values.
Results may differ from a plain program's by a relative error of at most 0.0001.
Values sent between devices are 32-bit elements; how exact they have to be, the bound alone decides.
A program may use at most 64 MiB of HBM per device.

v0:
```python
import jax
import jax.numpy as jnp
from jax import lax
from jax.sharding import PartitionSpec as P

SEG = 256
STEPS = 4


flow_rate = 0.035
drain_rate = 0.4


def with_halo(block, sides, width):
    for axis, dim in sides:
        count = lax.axis_size(axis)
        forward = [(i, i + 1) for i in range(count - 1)]
        backward = [(target, source) for source, target in forward]
        low = lax.ppermute(
            lax.slice_in_dim(block, block.shape[dim] - width, None, axis=dim), axis, forward
        )
        high = lax.ppermute(lax.slice_in_dim(block, 0, width, axis=dim), axis, backward)
        block = jnp.concatenate([low, block, high], axis=dim)
    return block


def entering(x, axis, combine, identity):
    size, index = (lax.axis_size(axis), lax.axis_index(axis))
    everything = jax.tree.map(lambda part: lax.all_gather(part, axis), x)
    start = jax.tree.map(
        lambda part, zero: jnp.broadcast_to(jnp.asarray(zero, part.dtype), part.shape), x, identity
    )

    def lap(k, before):
        reached = k < index
        new = combine(before, jax.tree.map(lambda part: part[k], everything))
        return jax.tree.map(lambda a, b: jnp.where(reached, a, b), new, before)

    return lax.fori_loop(0, size, lap, start)


def mobility(water, inv_n):
    root = jnp.cbrt(water)
    return water * root * root * inv_n


def compose(earlier, later):
    return (later[0] * earlier[0], later[0] * earlier[1] + later[1])


def shards(
    depth,
    bed,
    rain,
    rough_class,
    class_n,
    contact_seg,
    contact_lake,
    lake_slot,
    storage,
    area,
    release,
    upstream_link,
):
    members, row_count, col_count = depth.shape
    tiles_count = lax.axis_size("tiles")
    tile_index = lax.axis_index("tiles")
    lake_dev = storage.shape[1]
    per_row = col_count // SEG
    classes = jnp.arange(class_n.shape[0], dtype=jnp.int32)
    inv_n = jnp.sum(
        jnp.where(rough_class[None] == classes[:, None, None], (1.0 / class_n)[:, None, None], 0.0),
        axis=0,
    )
    face_index = tile_index * row_count + jnp.arange(row_count + 1)
    face_mask = ((face_index > 0) & (face_index < tiles_count * row_count)).astype(jnp.float32)[
        None, :, None
    ]
    segments = contact_seg.reshape(-1)
    bed_seg = bed.reshape(row_count * per_row, SEG)
    bed_contact = bed_seg[segments][None]
    linked = upstream_link.astype(jnp.float32)
    scale_a = jnp.broadcast_to(release * linked, (members, lake_dev))
    zero_col = jnp.zeros((members, row_count, 1), jnp.float32)
    water = depth
    pool_store = storage
    outflow_sum = jnp.zeros_like(storage)
    for routing_step in range(STEPS):
        surface = bed[None] + water
        mobile = mobility(water, inv_n[None])
        padded = with_halo(jnp.stack([surface, mobile]), (("tiles", 2),), 1)
        pad_surface = padded[0]
        pad_mobile = padded[1]
        across = (
            face_mask
            * 0.5
            * (pad_mobile[:, :-1] + pad_mobile[:, 1:])
            * (pad_surface[:, :-1] - pad_surface[:, 1:])
        )
        sideways = (
            0.5 * (mobile[..., :-1] + mobile[..., 1:]) * (surface[..., :-1] - surface[..., 1:])
        )
        inflow_net = (
            across[:, :-1]
            - across[:, 1:]
            + jnp.concatenate([zero_col, sideways], -1)
            - jnp.concatenate([sideways, zero_col], -1)
        )
        wetted = water + flow_rate * inflow_net + rain
        levels_now = pool_store / area[None]
        wet_seg = wetted.reshape(members, row_count * per_row, SEG)
        wet_contact = wet_seg[:, segments]
        surf_contact = bed_contact + wet_contact
        send_rows = jnp.concatenate([surf_contact, wet_contact], axis=-1).reshape(
            members, tiles_count, -1, 2 * SEG
        )
        rows_in = lax.all_to_all(send_rows, "tiles", split_axis=1, concat_axis=1, tiled=True)
        lake_ids = lax.all_to_all(contact_lake, "tiles", split_axis=1, concat_axis=1, tiled=True)
        live_mask = lake_ids >= 0
        position = jnp.where(
            live_mask, lake_slot[jnp.maximum(lake_ids, 0)] - tile_index * lake_dev, 0
        )
        pool_level = levels_now[:, position[0]]
        excess = jnp.maximum(rows_in[..., :SEG] - pool_level[..., None], 0.0)
        taken_water = (
            drain_rate
            * rows_in[..., SEG:]
            * excess
            / (1.0 + excess)
            * live_mask.astype(jnp.float32)[..., None]
        )
        returned = lax.all_to_all(taken_water, "tiles", split_axis=1, concat_axis=1, tiled=True)
        returned, slot_sums, owner_pos = (
            returned,
            jnp.sum(taken_water, axis=-1),
            jnp.where(live_mask, position, -1),
        )
        water = (
            wet_seg.at[:, segments]
            .add(-returned.reshape(members, -1, SEG))
            .reshape(members, row_count, col_count)
        )
        one_hot = (owner_pos.reshape(-1)[:, None] == jnp.arange(lake_dev)[None, :]).astype(
            jnp.float32
        )
        lateral = (
            jnp.dot(slot_sums.reshape(members, -1), one_hot, precision=lax.Precision.HIGHEST) / SEG
        )
        scale_b = release[None] * (pool_store + lateral)
        identity = (
            jnp.ones((members, lake_dev), jnp.float32),
            jnp.zeros((members, lake_dev), jnp.float32),
        )
        prefix_a, from_above = entering((scale_a, scale_b), "tiles", compose, identity)
        released = scale_a * from_above + scale_b
        pool_store = pool_store + lateral + linked[None] * from_above - released
        outflow_sum = outflow_sum + released
    ens_total = lax.psum(jnp.sum(outflow_sum, axis=0), "ens")
    ens_outflow = ens_total / (members * lax.axis_size("ens"))
    return (water, pool_store, ens_outflow)


def solution(mesh):
    return jax.shard_map(
        shards,
        mesh=mesh,
        in_specs=(
            P("ens", "tiles", None),
            P("tiles", None),
            P("ens", "tiles", None),
            P("tiles", None),
            P(),
            P("tiles", None, None),
            P("tiles", None, None),
            P(),
            P("ens", "tiles"),
            P("tiles"),
            P("tiles"),
            P("tiles"),
        ),
        out_specs=(P("ens", "tiles", None), P("ens", "tiles"), P("tiles")),
        check_vma=False,
    )
```

profile of v0, /device:TPU:1, one launch (start us, length us, event | category | flops | bytes accessed | tf_op | source)
XLA Modules:
  0.0 581.6 jit_solution(17109282134929255538)
XLA Ops:
  2.1 9.4 %all-to-all-start.1 = ((s32[1,32,8]{2,0,1:T(1,128)}), s32[1,32,8]{2,0,1:T(1,128)S(1)}, u32[]{:S(2)}, u32[]{:S(2)}) async-start(s32[1,32,8]{2,0,1:T(1,128)} %copy.95), calls=%async_computation.1 | async-start | bytes 32768 | tf_op jit(solution)/shard_map/all_to_all | solution.py:118
  12.2 3.0 select_reduce_fusion
  15.3 3.4 broadcast_add_fusion.6
  20.2 3.5 collective-permute-start
  23.7 2.1 collective-permute-start.1
  25.9 2.5 fusion.40
  31.7 2.9 pad_maximum_fusion
  37.9 2.1 fusion.46
  40.0 2.7 reshape.275
  42.7 4.5 copy.99
  47.2 2.8 gather_fusion.1
  51.9 8.5 %all-to-all-start = ((f32[2,32,8,512]{3,0,2,1:T(2,128)}), f32[2,32,8,512]{3,0,2,1:T(2,128)S(1)}, u32[]{:S(2)}, u32[]{:S(2)}) async-start(f32[2,32,8,512]{3,0,2,1:T(2,128)} %pad_maximum_fusion.4), calls=%async_computation | async-start | bytes 2097152 | tf_op jit(solution)/shard_map/all_to_all | solution.py:117
  63.8 13.7 %all-to-all-done = f32[2,32,8,512]{3,0,2,1:T(2,128)S(1)} async-done(((f32[2,32,8,512]{3,0,2,1:T(2,128)}), f32[2,32,8,512]{3,0,2,1:T(2,128)S(1)}, u32[]{:S(2)}, u32[]{:S(2)}) %all-to-all-start) | async-done | bytes 1048608 | tf_op jit(solution)/shard_map/all_to_all | solution.py:117
  77.5 3.2 fusion.82
  80.7 3.9 all-to-all-start.2
  85.4 66.1 %all-reduce.8 = f32[1280]{0:T(1024)S(1)} all-reduce(f32[1280]{0:T(1024)S(1)} %get-tuple-element.507), channel_id=3, replica_groups=mesh['tiles'=32,'ens'=4] {'tiles'}, use_global_device_ids=true, to_apply=%add.8 | all-reduce | flops 1280 | bytes 10240
  152.8 23.6 %all-gather.5 = f32[32,2,40]{2,1,0:T(2,128)S(1)} all-gather(f32[1,2,40]{2,1,0:T(2,128)S(1)} %multiply_bitcast_fusion.3), channel_id=4, replica_groups=mesh['tiles'=32,'ens'=4] {'tiles'}, dimensions={0}, use_global_device_ids=true | all-gather | bytes 10560 | tf_op jit(solution)/shard_map/all_gather | solution.py:29
  176.7 27.6 %scatter_fusion = f32[2,1024,256]{2,0,1:T(2,128)} fusion(f32[2,1024,256]{2,0,1:T(2,128)} %copy.99, s32[256]{0:T(256)S(1)} %bitcast.160, f32[256,2,256]{2,1,0:T(2,128)S(1)} %bitcast.150), kind=kCustom, calls=%fused_computation.10 | custom fusion | flops 131072 | bytes 1573888 | tf_op jit(solution)/shard_map/scatter-add | solution.py:140
  204.3 3.1 copy.100
  207.4 2.7 reshape.278
  210.1 2.8 reshape.279
  212.9 3.4 broadcast_add_fusion.2
  216.7 4.6 collective-permute-start.2
  226.2 2.8 collective-permute-done.3
  234.2 2.7 reshape.280
  236.9 4.5 copy.105
  241.5 2.8 gather_fusion.4
  246.2 8.4 %all-to-all-start.3 = ((f32[2,32,8,512]{3,0,2,1:T(2,128)}), f32[2,32,8,512]{3,0,2,1:T(2,128)S(1)}, u32[]{:S(2)}, u32[]{:S(2)}) async-start(f32[2,32,8,512]{3,0,2,1:T(2,128)} %pad_maximum_fusion.5), calls=%async_computation.3 | async-start | bytes 2097152 | tf_op jit(solution)/shard_map/all_to_all | solution.py:117
  257.4 14.3 %all-to-all-done.3 = f32[2,32,8,512]{3,0,2,1:T(2,128)S(1)} async-done(((f32[2,32,8,512]{3,0,2,1:T(2,128)}), f32[2,32,8,512]{3,0,2,1:T(2,128)S(1)}, u32[]{:S(2)}, u32[]{:S(2)}) %all-to-all-start.3) | async-done | bytes 1048608 | tf_op jit(solution)/shard_map/all_to_all | solution.py:117
  271.7 3.2 fusion.79
  274.9 3.9 all-to-all-start.4
  280.1 26.4 %all-gather.6 = f32[32,2,40]{2,1,0:T(2,128)S(1)} all-gather(f32[1,2,40]{2,1,0:T(2,128)S(1)} %multiply_bitcast_fusion.2), channel_id=5, replica_groups=mesh['tiles'=32,'ens'=4] {'tiles'}, dimensions={0}, use_global_device_ids=true | all-gather | bytes 10560 | tf_op jit(solution)/shard_map/all_gather | solution.py:29
  306.7 27.6 %scatter_fusion.1 = f32[2,1024,256]{2,0,1:T(2,128)} fusion(f32[2,1024,256]{2,0,1:T(2,128)} %copy.105, s32[256]{0:T(256)S(1)} %bitcast.161, f32[256,2,256]{2,1,0:T(2,128)S(1)} %bitcast.151), kind=kCustom, calls=%fused_computation.11 | custom fusion | flops 131072 | bytes 1573888 | tf_op jit(solution)/shard_map/scatter-add | solution.py:140
  334.3 3.1 copy.106
  337.4 2.7 reshape.282
  340.1 2.8 reshape.283
  342.9 3.4 broadcast_add_fusion.1
  348.8 2.4 collective-permute-start.5
  354.2 2.3 collective-permute-done.5
  361.8 2.7 reshape.284
  364.6 4.5 copy.111
  369.1 2.8 gather_fusion.6
  373.8 7.9 %all-to-all-start.5 = ((f32[2,32,8,512]{3,0,2,1:T(2,128)}), f32[2,32,8,512]{3,0,2,1:T(2,128)S(1)}, u32[]{:S(2)}, u32[]{:S(2)}) async-start(f32[2,32,8,512]{3,0,2,1:T(2,128)} %pad_maximum_fusion.6), calls=%async_computation.5 | async-start | bytes 2097152 | tf_op jit(solution)/shard_map/all_to_all | solution.py:117
  384.5 14.3 %all-to-all-done.5 = f32[2,32,8,512]{3,0,2,1:T(2,128)S(1)} async-done(((f32[2,32,8,512]{3,0,2,1:T(2,128)}), f32[2,32,8,512]{3,0,2,1:T(2,128)S(1)}, u32[]{:S(2)}, u32[]{:S(2)}) %all-to-all-start.5) | async-done | bytes 1048608 | tf_op jit(solution)/shard_map/all_to_all | solution.py:117
  398.8 3.2 fusion.77
  402.1 3.9 all-to-all-start.6
  407.2 26.3 %all-gather.7 = f32[32,2,40]{2,1,0:T(2,128)S(1)} all-gather(f32[1,2,40]{2,1,0:T(2,128)S(1)} %multiply_bitcast_fusion.1), channel_id=6, replica_groups=mesh['tiles'=32,'ens'=4] {'tiles'}, dimensions={0}, use_global_device_ids=true | all-gather | bytes 10560 | tf_op jit(solution)/shard_map/all_gather | solution.py:29
  433.9 27.6 %scatter_fusion.2 = f32[2,1024,256]{2,0,1:T(2,128)} fusion(f32[2,1024,256]{2,0,1:T(2,128)} %copy.111, s32[256]{0:T(256)S(1)} %bitcast.162, f32[256,2,256]{2,1,0:T(2,128)S(1)} %bitcast.152), kind=kCustom, calls=%fused_computation.12 | custom fusion | flops 131072 | bytes 1573888 | tf_op jit(solution)/shard_map/scatter-add | solution.py:140
  461.4 3.1 copy.112
  464.5 2.7 reshape.286
  467.3 2.8 reshape.287
  470.0 3.4 broadcast_add_fusion
  475.9 2.4 collective-permute-start.7
  481.4 2.3 collective-permute-done.7
  486.9 2.2 fusion.25
  489.0 2.7 reshape.288
  491.8 3.2 copy.117
  498.1 8.0 %all-to-all-start.7 = ((f32[2,32,8,512]{3,0,2,1:T(2,128)}), f32[2,32,8,512]{3,0,2,1:T(2,128)S(1)}, u32[]{:S(2)}, u32[]{:S(2)}) async-start(f32[2,32,8,512]{3,0,2,1:T(2,128)} %pad_maximum_fusion.7), calls=%async_computation.7 | async-start | bytes 2097152 | tf_op jit(solution)/shard_map/all_to_all | solution.py:117
  508.3 14.9 %all-to-all-done.7 = f32[2,32,8,512]{3,0,2,1:T(2,128)S(1)} async-done(((f32[2,32,8,512]{3,0,2,1:T(2,128)}), f32[2,32,8,512]{3,0,2,1:T(2,128)S(1)}, u32[]{:S(2)}, u32[]{:S(2)}) %all-to-all-start.7) | async-done | bytes 1048608 | tf_op jit(solution)/shard_map/all_to_all | solution.py:117
  525.2 4.0 all-to-all-start.8
  529.1 27.6 %all-gather.8 = f32[32,2,40]{2,1,0:T(2,128)S(1)} all-gather(f32[1,2,40]{2,1,0:T(2,128)S(1)} %multiply_bitcast_fusion), channel_id=7, replica_groups=mesh['tiles'=32,'ens'=4] {'tiles'}, dimensions={0}, use_global_device_ids=true | all-gather | bytes 10560 | tf_op jit(solution)/shard_map/all_gather | solution.py:29
  558.6 8.7 %psum.7 = f32[40]{0:T(128)S(1)} all-reduce(f32[40]{0:T(128)S(1)} %get-tuple-element.543), channel_id=1, replica_groups=mesh['tiles'=32,'ens'=4] {'ens'}, use_global_device_ids=true, to_apply=%region_18.19 | all-reduce | flops 40 | bytes 320 | tf_op jit(solution)/shard_map/psum | solution.py:158
  568.1 8.9 %scatter_fusion.3 = f32[2,1024,256]{2,0,1:T(2,128)S(1)} fusion(f32[2,1024,256]{2,0,1:T(2,128)S(1)} %copy.117, s32[256]{0:T(256)S(1)} %bitcast.163, f32[256,2,256]{2,1,0:T(2,128)S(1)} %bitcast.149), kind=kCustom, calls=%fused_computation.13 | custom fusion | flops 131072 | bytes 1573888 | tf_op jit(solution)/shard_map/scatter-add | solution.py:140
  578.4 2.7 reshape.290
  (306 shorter events, 72.3 us)
Async XLA Ops:
  0.6 59.8 %copy-start = (s32[1280]{0:T(1024)S(1)}, s32[1280]{0:T(1024)}, u32[]{:S(2)}) copy-start(s32[1280]{0:T(1024)} %param.27) | copy-start | bytes 15364
  0.6 14.6 %copy-start.2 = (f32[16,16384]{1,0:T(8,128)S(1)}, f32[16,16384]{1,0:T(8,128)}, u32[]{:S(2)}) copy-start(f32[16,16384]{1,0:T(8,128)} %param.21) | copy-start | bytes 3145732
  2.1 29.2 %all-to-all-start.1 = ((s32[1,32,8]{2,0,1:T(1,128)}), s32[1,32,8]{2,0,1:T(1,128)S(1)}, u32[]{:S(2)}, u32[]{:S(2)}) async-start(s32[1,32,8]{2,0,1:T(1,128)} %copy.95), calls=%async_computation.1 | async-start | bytes 32768 | tf_op jit(solution)/shard_map/all_to_all | solution.py:118
  18.7 7.2 %copy-start.3 = (f32[2,16,16384]{2,1,0:T(8,128)}, f32[2,16,16384]{2,1,0:T(8,128)S(1)}, u32[]{:S(2)}) copy-start(f32[2,16,16384]{2,1,0:T(8,128)S(1)} %get-tuple-element.541) | copy-start | bytes 6291460
  18.7 7.2 %copy-start.4 = (f32[2,16,16384]{2,1,0:T(8,128)}, f32[2,16,16384]{2,1,0:T(8,128)S(1)}, u32[]{:S(2)}) copy-start(f32[2,16,16384]{2,1,0:T(8,128)S(1)} %get-tuple-element.542) | copy-start | bytes 6291460
  20.2 11.2 %collective-permute-start = (f32[2,2,1,16384]{3,2,1,0:T(1,128)}, f32[2,2,1,16384]{3,2,1,0:T(1,128)}, u32[]{:S(2)}, u32[]{:S(2)}) collective-permute-start(f32[2,2,1,16384]{3,2,1,0:T(1,128)} %get-tuple-element.527), channel_id=1, source_target_pairs={{0,4},{4,8},{8,12},{12,16},{16,20},{20,24},{24,28},{28,32},{32,36}... | collective-permute-start | bytes 786440 | tf_op jit(solution)/shard_map/ppermute | solution.py:19
  23.7 8.0 %collective-permute-start.1 = (f32[2,2,1,16384]{3,2,1,0:T(1,128)}, f32[2,2,1,16384]{3,2,1,0:T(1,128)}, u32[]{:S(2)}, u32[]{:S(2)}) collective-permute-start(f32[2,2,1,16384]{3,2,1,0:T(1,128)} %get-tuple-element.528), channel_id=1, source_target_pairs={{4,0},{8,4},{12,8},{16,12},{20,16},{24,20},{28,24},{32,28},{36,32}... | collective-permute-start | bytes 786440 | tf_op jit(solution)/shard_map/ppermute | solution.py:22
  25.9 2.6 copy-start.32
  25.9 2.7 copy-start.25
  25.9 2.7 copy-start.31
  28.4 0.7 copy-start.34
  28.7 201.9 %copy-start.22 = (f32[17]{0:T(128)}, f32[17]{0:T(128)S(1)}, u32[]{:S(2)}) copy-start(f32[17]{0:T(128)S(1)} %and_select_fusion) | copy-start | bytes 208
  35.1 1.6 copy-start.5
  35.1 2.2 copy-start.12
  35.1 2.8 copy-start.13
  51.9 25.5 %all-to-all-start = ((f32[2,32,8,512]{3,0,2,1:T(2,128)}), f32[2,32,8,512]{3,0,2,1:T(2,128)S(1)}, u32[]{:S(2)}, u32[]{:S(2)}) async-start(f32[2,32,8,512]{3,0,2,1:T(2,128)} %pad_maximum_fusion.4), calls=%async_computation | async-start | bytes 2097152 | tf_op jit(solution)/shard_map/all_to_all | solution.py:117
  62.2 22.5 %copy-start.14 = (f32[40]{0:T(128)S(1)}, f32[40]{0:T(128)}, u32[]{:S(2)}) copy-start(f32[40]{0:T(128)} %param.30) | copy-start | bytes 484
  62.2 22.5 %copy-start.33 = (s32[40]{0:T(128)S(1)}, s32[40]{0:T(128)}, u32[]{:S(2)}) copy-start(s32[40]{0:T(128)} %param.31) | copy-start | bytes 484
  80.7 95.7 %all-to-all-start.2 = ((f32[2,32,8,256]{3,0,2,1:T(2,128)}), f32[2,32,8,256]{3,0,2,1:T(2,128)S(1)}, u32[]{:S(2)}, u32[]{:S(2)}) async-start(f32[2,32,8,256]{3,0,2,1:T(2,128)} %get-tuple-element.512), calls=%async_computation.2 | async-start | bytes 1048576 | tf_op jit(solution)/shard_map/all_to_all | solution.py:132
  84.8 171.1 %copy-start.19 = (f32[40]{0:T(128)}, f32[40]{0:T(128)S(1)}, u32[]{:S(2)}) copy-start(f32[40]{0:T(128)S(1)} %get-tuple-element.508) | copy-start | bytes 484
  216.3 6.9 %copy-start.10 = (f32[2,16,16384]{2,1,0:T(8,128)S(1)}, f32[2,16,16384]{2,1,0:T(8,128)}, u32[]{:S(2)}) copy-start(f32[2,16,16384]{2,1,0:T(8,128)} %reshape.278) | copy-start | bytes 6291460
  216.7 9.5 %collective-permute-start.2 = (f32[2,2,1,16384]{3,2,1,0:T(1,128)S(1)}, f32[2,2,1,16384]{3,2,1,0:T(1,128)S(1)}, u32[]{:S(2)}, u32[]{:S(2)}) collective-permute-start(f32[2,2,1,16384]{3,2,1,0:T(1,128)S(1)} %get-tuple-element.525), channel_id=1, source_target_pairs={{0,4},{4,8},{8,12},{12,16},{16,20},{20,24},{24,28},{28,32},{32,36}... | collective-permute-start | bytes 786440 | tf_op jit(solution)/shard_map/ppermute | solution.py:19
  221.3 7.7 %collective-permute-start.3 = (f32[2,2,1,16384]{3,2,1,0:T(1,128)S(1)}, f32[2,2,1,16384]{3,2,1,0:T(1,128)S(1)}, u32[]{:S(2)}, u32[]{:S(2)}) collective-permute-start(f32[2,2,1,16384]{3,2,1,0:T(1,128)S(1)} %get-tuple-element.526), channel_id=1, source_target_pairs={{4,0},{8,4},{12,8},{16,12},{20,16},{24,20},{28,24},{32,28},{36,32}... | collective-permute-start | bytes 786440 | tf_op jit(solution)/shard_map/ppermute | solution.py:22
  230.6 1.6 copy-start.6
  244.6 11.3 %copy-start.28 = (f32[40]{0:T(128)S(1)}, f32[40]{0:T(128)}, u32[]{:S(2)}) copy-start(f32[40]{0:T(128)} %convert_element_type.3) | copy-start | bytes 484
  246.2 25.5 %all-to-all-start.3 = ((f32[2,32,8,512]{3,0,2,1:T(2,128)}), f32[2,32,8,512]{3,0,2,1:T(2,128)S(1)}, u32[]{:S(2)}, u32[]{:S(2)}) async-start(f32[2,32,8,512]{3,0,2,1:T(2,128)} %pad_maximum_fusion.5), calls=%async_computation.3 | async-start | bytes 2097152 | tf_op jit(solution)/shard_map/all_to_all | solution.py:117
  274.9 31.5 %all-to-all-start.4 = ((f32[2,32,8,256]{3,0,2,1:T(2,128)}), f32[2,32,8,256]{3,0,2,1:T(2,128)S(1)}, u32[]{:S(2)}, u32[]{:S(2)}) async-start(f32[2,32,8,256]{3,0,2,1:T(2,128)} %get-tuple-element.504), calls=%async_computation.4 | async-start | bytes 1048576 | tf_op jit(solution)/shard_map/all_to_all | solution.py:132
  280.1 103.0 %copy-start.15 = (f32[2,40]{1,0:T(2,128)}, f32[2,40]{1,0:T(2,128)S(1)}, u32[]{:S(2)}) copy-start(f32[2,40]{1,0:T(2,128)S(1)} %fusion.49) | copy-start | bytes 964
  346.3 4.9 copy-start.11
  346.7 7.5 %collective-permute-start.4 = (f32[2,2,1,16384]{3,2,1,0:T(1,128)S(1)}, f32[2,2,1,16384]{3,2,1,0:T(1,128)S(1)}, u32[]{:S(2)}, u32[]{:S(2)}) collective-permute-start(f32[2,2,1,16384]{3,2,1,0:T(1,128)S(1)} %get-tuple-element.523), channel_id=1, source_target_pairs={{0,4},{4,8},{8,12},{12,16},{16,20},{20,24},{24,28},{28,32},{32,36}... | collective-permute-start | bytes 786440 | tf_op jit(solution)/shard_map/ppermute | solution.py:19
  348.8 7.7 %collective-permute-start.5 = (f32[2,2,1,16384]{3,2,1,0:T(1,128)S(1)}, f32[2,2,1,16384]{3,2,1,0:T(1,128)S(1)}, u32[]{:S(2)}, u32[]{:S(2)}) collective-permute-start(f32[2,2,1,16384]{3,2,1,0:T(1,128)S(1)} %get-tuple-element.524), channel_id=1, source_target_pairs={{4,0},{8,4},{12,8},{16,12},{20,16},{24,20},{28,24},{32,28},{36,32}... | collective-permute-start | bytes 786440 | tf_op jit(solution)/shard_map/ppermute | solution.py:22
  357.6 0.6 copy-start.23
  358.2 1.6 copy-start.7
  372.2 10.8 %copy-start.20 = (f32[40]{0:T(128)S(1)}, f32[40]{0:T(128)}, u32[]{:S(2)}) copy-start(f32[40]{0:T(128)} %copy-done.19) | copy-start | bytes 484
  372.2 10.8 %copy-start.26 = (f32[40]{0:T(128)S(1)}, f32[40]{0:T(128)}, u32[]{:S(2)}) copy-start(f32[40]{0:T(128)} %param.29) | copy-start | bytes 484
  372.3 10.8 %copy-start.29 = (f32[40]{0:T(128)S(1)}, f32[40]{0:T(128)}, u32[]{:S(2)}) copy-start(f32[40]{0:T(128)} %convert_element_type.3) | copy-start | bytes 484
  373.8 25.0 %all-to-all-start.5 = ((f32[2,32,8,512]{3,0,2,1:T(2,128)}), f32[2,32,8,512]{3,0,2,1:T(2,128)S(1)}, u32[]{:S(2)}, u32[]{:S(2)}) async-start(f32[2,32,8,512]{3,0,2,1:T(2,128)} %pad_maximum_fusion.6), calls=%async_computation.5 | async-start | bytes 2097152 | tf_op jit(solution)/shard_map/all_to_all | solution.py:117
  402.1 31.5 %all-to-all-start.6 = ((f32[2,32,8,256]{3,0,2,1:T(2,128)}), f32[2,32,8,256]{3,0,2,1:T(2,128)S(1)}, u32[]{:S(2)}, u32[]{:S(2)}) async-start(f32[2,32,8,256]{3,0,2,1:T(2,128)} %get-tuple-element.500), calls=%async_computation.6 | async-start | bytes 1048576 | tf_op jit(solution)/shard_map/all_to_all | solution.py:132
  407.2 100.1 %copy-start.17 = (f32[2,40]{1,0:T(2,128)}, f32[2,40]{1,0:T(2,128)S(1)}, u32[]{:S(2)}) copy-start(f32[2,40]{1,0:T(2,128)S(1)} %fusion.48) | copy-start | bytes 964
  473.5 4.9 copy-start.9
  473.9 7.5 %collective-permute-start.6 = (f32[2,2,1,16384]{3,2,1,0:T(1,128)S(1)}, f32[2,2,1,16384]{3,2,1,0:T(1,128)S(1)}, u32[]{:S(2)}, u32[]{:S(2)}) collective-permute-start(f32[2,2,1,16384]{3,2,1,0:T(1,128)S(1)} %get-tuple-element.521), channel_id=1, source_target_pairs={{0,4},{4,8},{8,12},{12,16},{16,20},{20,24},{24,28},{28,32},{32,36}... | collective-permute-start | bytes 786440 | tf_op jit(solution)/shard_map/ppermute | solution.py:19
  475.9 7.7 %collective-permute-start.7 = (f32[2,2,1,16384]{3,2,1,0:T(1,128)S(1)}, f32[2,2,1,16384]{3,2,1,0:T(1,128)S(1)}, u32[]{:S(2)}, u32[]{:S(2)}) collective-permute-start(f32[2,2,1,16384]{3,2,1,0:T(1,128)S(1)} %get-tuple-element.522), channel_id=1, source_target_pairs={{4,0},{8,4},{12,8},{16,12},{20,16},{24,20},{28,24},{32,28},{36,32}... | collective-permute-start | bytes 786440 | tf_op jit(solution)/shard_map/ppermute | solution.py:22
  484.7 0.6 copy-start.24
  485.3 1.6 copy-start.8
  496.5 10.9 %copy-start.21 = (f32[40]{0:T(128)S(1)}, f32[40]{0:T(128)}, u32[]{:S(2)}) copy-start(f32[40]{0:T(128)} %copy-done.19) | copy-start | bytes 484
  496.5 10.9 %copy-start.27 = (f32[40]{0:T(128)S(1)}, f32[40]{0:T(128)}, u32[]{:S(2)}) copy-start(f32[40]{0:T(128)} %param.29) | copy-start | bytes 484
  496.6 10.8 %copy-start.30 = (f32[40]{0:T(128)S(1)}, f32[40]{0:T(128)}, u32[]{:S(2)}) copy-start(f32[40]{0:T(128)} %convert_element_type.3) | copy-start | bytes 484
  498.1 25.0 %all-to-all-start.7 = ((f32[2,32,8,512]{3,0,2,1:T(2,128)}), f32[2,32,8,512]{3,0,2,1:T(2,128)S(1)}, u32[]{:S(2)}, u32[]{:S(2)}) async-start(f32[2,32,8,512]{3,0,2,1:T(2,128)} %pad_maximum_fusion.7), calls=%async_computation.7 | async-start | bytes 2097152 | tf_op jit(solution)/shard_map/all_to_all | solution.py:117
  506.1 51.9 %copy-start.16 = (f32[2,40]{1,0:T(2,128)S(1)}, f32[2,40]{1,0:T(2,128)}, u32[]{:S(2)}) copy-start(f32[2,40]{1,0:T(2,128)} %copy-done.15) | copy-start | bytes 964
  507.4 50.5 %copy-start.18 = (f32[2,40]{1,0:T(2,128)S(1)}, f32[2,40]{1,0:T(2,128)}, u32[]{:S(2)}) copy-start(f32[2,40]{1,0:T(2,128)} %copy-done.17) | copy-start | bytes 964
  525.2 42.6 %all-to-all-start.8 = ((f32[2,32,8,256]{3,0,2,1:T(2,128)}), f32[2,32,8,256]{3,0,2,1:T(2,128)S(1)}, u32[]{:S(2)}, u32[]{:S(2)}) async-start(f32[2,32,8,256]{3,0,2,1:T(2,128)} %get-tuple-element.496), calls=%async_computation.8 | async-start | bytes 1048576 | tf_op jit(solution)/shard_map/all_to_all | solution.py:132
  576.9 4.3 copy-start.1
where the time goes:
time: 590 us; the launch traced here: 582 us
  blocking collectives  179 us (30%)
  other arithmetic  165 us (28%)
  local copies, waits for them, and re-layouts  84.8 us (14%)
  starting transfers between devices  79.1 us (13%)
  waiting for transfers between devices  64.7 us (11%)
    all_gather x4, blocking collectives, entering(): everything = jax.tree.map(lambda part: lax.all_gather(part, axis), x)  104 us
    scatter-add x4, other arithmetic, shards(): water = wet_seg.at[:, segments].add(-returned.reshape(members, -1, SEG))....  91.5 us
    unnamed x1, blocking collectives  66.1 us
    all_to_all x4, waiting for transfers between devices, shards(): lax.all_to_all(send_rows, 'tiles', split_axis=1, concat_axis=1, tiled=True)  57.1 us
    all_to_all x4, starting transfers between devices, shards(): lax.all_to_all(send_rows, 'tiles', split_axis=1, concat_axis=1, tiled=True)  32.8 us
    reshape x8, local copies, waits for them, and re-layouts, shards(): wet_seg = wetted.reshape(members, row_count * per_row, SEG)  27.7 us
    reshape x7, local copies, waits for them, and re-layouts, shards(): water = wet_seg.at[:, segments].add(-returned.reshape(members, -1, SEG))....  19.3 us
    all_to_all x4, starting transfers between devices, shards(): lax.all_to_all(taken_water, 'tiles', split_axis=1, concat_axis=1, tiled=T...  15.8 us
  transfers between devices with their start and end apart: 17, of which 8 were waited for; matrix products, arithmetic and copies ran while one was open for 6% of the time, Pallas kernels for 0%

commit v1 on v0

v1 whole, which is shorter than its diff:
```python
import jax
import jax.numpy as jnp
from jax import lax
from jax.experimental import pallas as pl
from jax.experimental.pallas import tpu as pltpu
from jax.sharding import PartitionSpec as P

STEPS = 4
TILES = 32
ENS = 4
MEMB = 2
ROWS = 16
COLS = 16384
BLOCKS = 16
LAKE_DEV = 40
FLOW = 0.035
DRAIN = 0.4
FAR = 3.0e38
MESH = pl.DeviceIdType.MESH
F32 = jnp.float32
I32 = jnp.int32


def iota(axis):
    return lax.broadcasted_iota(I32, (8, 128), axis)


def merge(a, b, index, bit, axis):
    odd = (index & bit) != 0
    return jnp.where(odd, b, a) + pltpu.roll(jnp.where(odd, a, b), bit, axis)


def spread(row):
    return jnp.broadcast_to(row, (8, 128))


def lanes_of(table, index):
    return jnp.take_along_axis(table, index, axis=1)


def power(water):
    return water * jnp.exp2(jnp.log2(jnp.abs(water)) * (2.0 / 3.0))


def peer_offsets():
    near = {0: 0, 1: 1, 2: 2, 3: 1}
    found = [
        (z, x, c) for z in range(4) for x in range(4) for c in range(2) if (z, x, c) != (0, 0, 0)
    ]
    return sorted(found, key=lambda o: (-near[o[0]] - near[o[1]], o))


def kernel(
    depth, bed_in, rain_in, rough, class_n, contact_seg, contact_lake, lake_slot,
    storage, area, release, link,
    new_depth, new_storage, ens_outflow,
    wat, rain, bed, ivn, wet, rgh,
    seg_s, lake_s, slot_s, cls_v, sto_v, are_v, rel_v, lnk_v,
    hello, greet, turn, pos, pool, outf, par,
    edge0, halo0, edge, halo, flux, part, msg, got, emsg, egot,
    lsem, psem, isem, ssem, rsem, hsend, hrecv, esend, erecv, osem,
):
    me = lax.axis_index("tiles")
    ye = lax.axis_index("ens")
    sub, lane = iota(0), iota(1)
    before, after = lax.rem(me + TILES - 1, TILES), lax.rem(me + 1, TILES)
    z, x, core = me // 8, (me // 2) % 4, me % 2
    peers = [
        (lax.rem(z + dz, 4) * 4 + lax.rem(x + dx, 4)) * 2 + lax.rem(core + dc, 2)
        for dz, dx, dc in peer_offsets()
    ]
    others = [lax.rem(ye + k, ENS) for k in range(1, ENS)]

    smalls = [
        (contact_seg, seg_s), (contact_lake, lake_s), (lake_slot, slot_s), (class_n, cls_v),
        (storage, sto_v), (area, are_v), (release, rel_v), (link, lnk_v),
    ]
    bigs = [(rough, rgh), (bed_in, bed), (depth, wat), (rain_in, rain)]
    loads = [pltpu.make_async_copy(a, b, lsem.at[i]) for i, (a, b) in enumerate(smalls + bigs)]
    for load in loads:
        load.start()

    barrier = pltpu.get_barrier_semaphore()
    for peer in peers:
        pl.semaphore_signal(barrier, inc=1, device_id={"tiles": peer}, device_id_type=MESH)
    for other in others:
        pl.semaphore_signal(barrier, inc=1, device_id={"ens": other}, device_id_type=MESH)

    for load in loads[: len(smalls)]:
        load.wait()

    seg_id = ((lane & 1) * 8 + sub) * 64 + (lane >> 1)
    contact_id = (lane & 31) * 8 + (sub >> 1) * 4 + (lane >> 5)

    def read_contacts(e, carry):
        code, from_seg, where_to = carry
        for c in range(8):
            seg = seg_s[0, e, c]
            lake = lake_s[0, e, c]
            live = lake >= 0
            place = slot_s[0, jnp.maximum(lake, 0)] - e * LAKE_DEV
            code = jnp.where(seg_id == seg, jnp.where(live, place * 32 + e, -1), code)
            mine = contact_id == e * 8 + c
            from_seg = jnp.where(mine, seg, from_seg)
            where_to = jnp.where(mine, jnp.where(live, place, -1), where_to)
        return code, from_seg, where_to

    none = jnp.full((8, 128), -1, I32)
    code, from_seg, where_to = lax.fori_loop(
        0, TILES, read_contacts, (none, jnp.zeros((8, 128), I32), none)
    )
    code_row, code_lane = code >> 7, code & 127
    src_sub = (from_seg >> 6) & 7
    src_lane = (from_seg & 63) * 2 + (from_seg >> 9)

    place_rows = where_to.astype(F32)
    hello[...] = jnp.zeros((8, 128), F32)
    hello[0:1, :] = place_rows[0:1, :]
    hello[1:2, :] = place_rows[2:3, :]
    hello[2:4, 0:LAKE_DEV] = sto_v[...]
    hello[4:5, 0:LAKE_DEV] = are_v[...]
    hello[5:6, 0:LAKE_DEV] = rel_v[...]
    hello[6:7, 0:LAKE_DEV] = lnk_v[...].astype(F32)

    pl.semaphore_wait(barrier, TILES - 1 + ENS - 1)
    for peer in peers:
        pltpu.make_async_remote_copy(
            hello, greet.at[me], psem, isem, device_id={"tiles": peer}, device_id_type=MESH
        ).start()
    pltpu.make_async_copy(hello, greet.at[me], isem).start()

    for load in loads[len(smalls):]:
        load.wait()
    inverse = (0.5 * FLOW) / cls_v[...]
    turn[...] = jnp.zeros((128, 128), F32)
    turn[0:1, 0:16] = inverse
    classes = spread(turn[0:1, :])

    def read_rough(i, carry):
        base = pl.multiple_of(i * 1024, 1024)
        for j in range(8):
            cols = pl.ds(base + j * 128, 128)
            for half in range(2):
                rows = slice(half * 8, half * 8 + 8)
                ivn[rows, cols] = lanes_of(classes, rgh[rows, cols])
            for side, row in ((0, 0), (1, 15)):
                edge0[side, 0, i, j:j + 1, :] = wat[0, row:row + 1, cols]
                edge0[side, 1, i, j:j + 1, :] = wat[1, row:row + 1, cols]
                edge0[side, 2, i, j:j + 1, :] = bed[row:row + 1, cols]
                edge0[side, 3, i, j:j + 1, :] = ivn[row:row + 1, cols]
        return carry

    lax.fori_loop(0, BLOCKS, read_rough, 0)

    def halo_copies(step):
        source, target = (edge0, halo0) if step == 0 else (edge.at[step - 1], halo.at[step - 1])
        return [
            pltpu.make_async_remote_copy(
                source.at[side], target.at[1 - side], hsend.at[step, side], hrecv.at[step, side],
                device_id={"tiles": (before, after)[side]}, device_id_type=MESH,
            )
            for side in (0, 1)
        ]

    def flows(step):
        mine, theirs = (edge0, halo0) if step == 0 else (edge.at[step - 1], halo.at[step - 1])
        inside = (me > 0, me < TILES - 1)

        def edge_flux(i, carry):
            for side in (0, 1):
                for m in range(MEMB):
                    w_own, w_far = mine[side, m, i], theirs[side, m, i]
                    s_own = w_own + edge0[side, 2, i]
                    s_far = w_far + halo0[side, 2, i]
                    m_own = power(w_own) * edge0[side, 3, i]
                    m_far = power(w_far) * halo0[side, 3, i]
                    value = (m_own + m_far) * ((s_far - s_own) if side == 0 else (s_own - s_far))
                    flux[side, m, i] = jnp.where(inside[side], value, 0.0)
            return carry

        lax.fori_loop(0, BLOCKS, edge_flux, 0)
        top, bottom = sub == 0, sub == 7
        first, last = lane == 0, lane == 127

        def block(i, carry):
            carry = list(carry)
            base = pl.multiple_of(i * 1024, 1024)
            for j in range(8):
                cols = pl.ds(base + j * 128, 128)
                done = pl.ds(base + j * 128, 128)
                beds = [bed[h * 8:h * 8 + 8, cols] for h in range(2)]
                invs = [ivn[h * 8:h * 8 + 8, cols] for h in range(2)]
                for m in range(MEMB):
                    w = [wat[m, h * 8:h * 8 + 8, cols] for h in range(2)]
                    s = [beds[h] + w[h] for h in range(2)]
                    mo = [power(w[h]) * invs[h] for h in range(2)]
                    s_dn = [pltpu.roll(v, 1, 0) for v in s]
                    m_dn = [pltpu.roll(v, 1, 0) for v in mo]
                    fv0 = jnp.where(
                        top, spread(flux[0, m, i, j:j + 1, :]), (m_dn[0] + mo[0]) * (s_dn[0] - s[0])
                    )
                    fv1 = (jnp.where(top, m_dn[0], m_dn[1]) + mo[1]) * (
                        jnp.where(top, s_dn[0], s_dn[1]) - s[1]
                    )
                    up0, up1 = pltpu.roll(fv0, 7, 0), pltpu.roll(fv1, 7, 0)
                    nv = [
                        fv0 - jnp.where(bottom, up1, up0),
                        fv1 - jnp.where(bottom, spread(flux[1, m, i, j:j + 1, :]), up1),
                    ]
                    for h in range(2):
                        at = (m * 2 + h) * 4
                        s_prev, m_prev, f_prev, sum_prev = carry[at:at + 4]
                        s_rt, m_rt = pltpu.roll(s[h], 1, 1), pltpu.roll(mo[h], 1, 1)
                        f = (jnp.where(first, m_prev, m_rt) + mo[h]) * (
                            jnp.where(first, s_prev, s_rt) - s[h]
                        )
                        f_lt = pltpu.roll(f, 127, 1)
                        wet[m, h * 8:h * 8 + 8, done] = sum_prev - jnp.where(last, f_lt, f_prev)
                        total = (w[h] + rain[m, h * 8:h * 8 + 8, cols]) + (nv[h] + f)
                        carry[at:at + 4] = [s_rt, m_rt, f_lt, total]
            return tuple(carry)

        zero = jnp.zeros((8, 128), F32)
        start = []
        for m in range(MEMB):
            for h in range(2):
                rows = slice(h * 8, h * 8 + 8)
                start += [bed[rows, 0:128] + wat[m, rows, 0:128], zero, zero, zero]
        carry = lax.fori_loop(0, BLOCKS, block, tuple(start))
        for m in range(MEMB):
            for h in range(2):
                f_prev, sum_prev = carry[(m * 2 + h) * 4 + 2:(m * 2 + h) * 4 + 4]
                wet[m, h * 8:h * 8 + 8, COLS:COLS + 128] = sum_prev - jnp.where(last, 0.0, f_prev)

    def drain(step, levels):
        found = [jnp.full((8, 128), FAR, F32) for _ in range(MEMB)]
        for j in range(LAKE_DEV // 4):
            here = code_row == j
            for m in range(MEMB):
                r = 2 * j + m
                row = spread(levels[r // 8][r % 8:r % 8 + 1, :])
                found[m] = jnp.where(here, lanes_of(row, code_lane), found[m])

        def block(i, carry):
            base = pl.multiple_of(i * 1024, 1024)
            shift = lax.rem(128 - i * 8, 128)
            beds = {}
            for m in range(MEMB):
                turned = pltpu.roll(found[m], shift, 1)
                leaves = []
                for g in range(4):
                    for h in range(2):
                        rows = slice(h * 8, h * 8 + 8)
                        level = spread(turned[:, 2 * g + h:2 * g + h + 1])
                        leaf = None
                        for j in (2 * g, 2 * g + 1):
                            cols = pl.ds(base + j * 128, 128)
                            w = wet[m, rows, pl.ds(base + j * 128 + 128, 128)]
                            excess = jnp.maximum((bed[rows, cols] + w) - level, 0.0)
                            taken = (DRAIN * w) * (excess / (1.0 + excess))
                            left = w - taken
                            wat[m, rows, cols] = left
                            if step < STEPS - 1:
                                r = 0 if h == 0 else 7
                                edge[step, h, m, i, j:j + 1, :] = left[r:r + 1, :]
                            leaf = taken if leaf is None else leaf + taken
                        leaves.append(leaf)
                for bit in (1, 2, 4):
                    leaves = [
                        merge(leaves[n], leaves[n + 1], lane, bit, 1)
                        for n in range(0, len(leaves), 2)
                    ]
                part[m, i] = leaves[0]
            return carry

        lax.fori_loop(0, BLOCKS, block, 0)
        sums = []
        for m in range(MEMB):
            leaves = [part[m, i] for i in range(BLOCKS)]
            for bit in (8, 16, 32, 64):
                leaves = [
                    merge(leaves[n], leaves[n + 1], lane, bit, 1) for n in range(0, len(leaves), 2)
                ]
            sums.append(leaves[0])
        return sums

    def tell(step, sums):
        picked = [jnp.zeros((8, 128), F32) for _ in range(MEMB)]
        for k in range(8):
            here = src_sub == k
            for m in range(MEMB):
                row = spread(sums[m][k:k + 1, :])
                picked[m] = jnp.where(here, lanes_of(row, src_lane), picked[m])
        msg[step] = jnp.where((sub & 1) == 0, picked[0], picked[1])[0:4, :]
        for peer in peers:
            pltpu.make_async_remote_copy(
                msg.at[step], got.at[step, me], ssem.at[step], rsem.at[step],
                device_id={"tiles": peer}, device_id_type=MESH,
            ).start()
        pltpu.make_async_copy(msg.at[step], got.at[step, me], rsem.at[step]).start()

    def hear(step):
        pltpu.make_async_copy(got.at[step], got.at[step], rsem.at[step]).wait()
        values = [
            jnp.concatenate([got[step, 2 * n], got[step, 2 * n + 1]], axis=0)
            for n in range(TILES // 2)
        ]
        places = [pos[n] for n in range(TILES // 2)]
        lateral = []
        for v in range(3):
            leaves = []
            for p in range(v * 16, min(v * 16 + 16, LAKE_DEV)):
                terms = [
                    jnp.where(places[n] == float(p), values[n], 0.0) for n in range(TILES // 2)
                ]
                while len(terms) > 1:
                    terms = [terms[n] + terms[n + 1] for n in range(0, len(terms), 2)]
                leaves.append(terms[0])
            for index, bit, axis in ((lane, 32, 1), (lane, 64, 1), (sub, 2, 0)):
                leaves = [
                    merge(leaves[n], leaves[n + 1], index, bit, axis)
                    for n in range(0, len(leaves), 2)
                ]
            if len(leaves) == 1:
                leaves.append(jnp.zeros((8, 128), F32))
            lateral.append(merge(leaves[0], leaves[1], sub, 4, 0) * (1.0 / 256.0))
        for v in range(3):
            rows = slice(v * 8, v * 8 + 8)
            held = pool[rows, :]
            out = par[1, rows, :] * (held + lateral[v])
            for stage, shift in ((3, 1), (4, 2), (5, 4), (6, 8)):
                out = out + par[stage, rows, :] * pltpu.roll(out, shift, 1)
            above = par[2, rows, :] * pltpu.roll(out, 1, 1)
            pool[rows, :] = held + lateral[v] + above - out
            outf[rows, :] = outf[rows, :] + out

    def level_now():
        return [pool[v * 8:v * 8 + 8, :] * par[0, v * 8:v * 8 + 8, :] for v in range(3)]

    for copy in halo_copies(0):
        copy.start()

    pltpu.make_async_copy(greet, greet, isem).wait()
    for n in range(TILES // 2):
        quarter = [
            spread(greet[2 * n + d, c:c + 1, :]) for d in range(2) for c in range(2)
        ]
        pos[n] = jnp.where(
            sub < 4,
            jnp.where(sub < 2, quarter[0], quarter[1]),
            jnp.where(sub < 6, quarter[2], quarter[3]),
        )
    for k in range(4):
        pick = (lane & 15) * 4 + k
        for b in range(4):
            tile = jnp.zeros((8, 128), F32)
            for kind in range(5):
                rows = greet[b * 8:b * 8 + 8, 2 + kind, :]
                tile = jnp.where((lane >> 4) == kind, lanes_of(rows, pick), tile)
            turn[k * 32 + b * 8:k * 32 + b * 8 + 8, :] = tile
    turn[...] = jnp.transpose(turn[...])
    pool[...] = jnp.zeros((24, 128), F32)
    outf[...] = jnp.zeros((24, 128), F32)
    par[0] = jnp.ones((24, 128), F32)
    par[1] = jnp.zeros((24, 128), F32)
    par[2] = jnp.zeros((24, 128), F32)
    for j in range(LAKE_DEV // 4):
        for m in range(MEMB):
            r = 2 * j + m
            pool[r:r + 1, :] = turn[16 * m + j:16 * m + j + 1, :]
            for kind in range(3):
                at = 32 + 16 * kind + j
                par[kind, r:r + 1, :] = turn[at:at + 1, :]
    for v in range(3):
        rows = slice(v * 8, v * 8 + 8)
        par[0, rows, :] = 1.0 / par[0, rows, :]
        chain = par[1, rows, :] * par[2, rows, :]
        for stage, shift in ((3, 1), (4, 2), (5, 4), (6, 8)):
            par[stage, rows, :] = chain
            chain = chain * pltpu.roll(chain, shift, 1)

    for step in range(STEPS):
        for copy in halo_copies(step):
            copy.wait_recv()
        flows(step)
        if step > 0:
            hear(step - 1)
        sums = drain(step, level_now())
        tell(step, sums)
        if step < STEPS - 1:
            for copy in halo_copies(step + 1):
                copy.start()
    store = pltpu.make_async_copy(wat, new_depth, osem)
    store.start()
    hear(STEPS - 1)

    pick = (lane & 3) * 32 + me
    own = [jnp.zeros((8, 128), F32) for _ in range(2)]
    for j in range(LAKE_DEV // 4):
        for m in range(MEMB):
            r = 2 * j + m
            here = (lane >> 2) == j
            own[0] = jnp.where(
                here & ((sub & 1) == m), lanes_of(spread(pool[r:r + 1, :]), pick), own[0]
            )
            own[1] = own[1] + jnp.where(here, lanes_of(spread(outf[r:r + 1, :]), pick), 0.0)
    emsg[...] = own[1]
    for k, other in enumerate(others):
        pltpu.make_async_remote_copy(
            emsg, egot.at[ye], esend, erecv, device_id={"ens": other}, device_id_type=MESH
        ).start()
    pltpu.make_async_copy(emsg, egot.at[ye], erecv).start()
    new_storage[...] = own[0][0:2, 0:LAKE_DEV]
    pltpu.make_async_copy(egot, egot, erecv).wait()
    total = (egot[0] + egot[1] + egot[2] + egot[3]) * (1.0 / (MEMB * ENS))
    ens_outflow[...] = total[0:1, 0:LAKE_DEV]

    store.wait()
    pltpu.make_async_copy(greet.at[1:], greet.at[1:], psem).wait()
    for step in range(STEPS):
        for copy in halo_copies(step):
            copy.wait_send()
        pltpu.make_async_copy(got.at[step, 1:], got.at[step, 1:], ssem.at[step]).wait()
    pltpu.make_async_copy(egot.at[1:], egot.at[1:], esend).wait()


def shards(
    depth, bed, rain, rough_class, class_n, contact_seg, contact_lake, lake_slot,
    storage, area, release, upstream_link,
):
    anywhere = pl.BlockSpec(memory_space=pl.ANY)
    vmem = pl.BlockSpec(memory_space=pltpu.VMEM)
    dma = pltpu.SemaphoreType.DMA
    water, pool, outflow = pl.pallas_call(
        kernel,
        out_shape=(
            jax.ShapeDtypeStruct((MEMB, ROWS, COLS), F32),
            jax.ShapeDtypeStruct((MEMB, LAKE_DEV), F32),
            jax.ShapeDtypeStruct((1, LAKE_DEV), F32),
        ),
        in_specs=[anywhere] * 12,
        out_specs=(anywhere, vmem, vmem),
        scratch_shapes=[
            pltpu.VMEM((MEMB, ROWS, COLS), F32),
            pltpu.VMEM((MEMB, ROWS, COLS), F32),
            pltpu.VMEM((ROWS, COLS), F32),
            pltpu.VMEM((ROWS, COLS), F32),
            pltpu.VMEM((MEMB, ROWS, COLS + 128), F32),
            pltpu.VMEM((ROWS, COLS), I32),
            pltpu.SMEM((1, TILES, 8), I32),
            pltpu.SMEM((1, TILES, 8), I32),
            pltpu.SMEM((1, TILES * LAKE_DEV), I32),
            pltpu.VMEM((1, 16), F32),
            pltpu.VMEM((MEMB, LAKE_DEV), F32),
            pltpu.VMEM((1, LAKE_DEV), F32),
            pltpu.VMEM((1, LAKE_DEV), F32),
            pltpu.VMEM((1, LAKE_DEV), I32),
            pltpu.VMEM((8, 128), F32),
            pltpu.VMEM((TILES, 8, 128), F32),
            pltpu.VMEM((128, 128), F32),
            pltpu.VMEM((TILES // 2, 8, 128), F32),
            pltpu.VMEM((24, 128), F32),
            pltpu.VMEM((24, 128), F32),
            pltpu.VMEM((7, 24, 128), F32),
            pltpu.VMEM((2, 4, BLOCKS, 8, 128), F32),
            pltpu.VMEM((2, 4, BLOCKS, 8, 128), F32),
            pltpu.VMEM((STEPS - 1, 2, MEMB, BLOCKS, 8, 128), F32),
            pltpu.VMEM((STEPS - 1, 2, MEMB, BLOCKS, 8, 128), F32),
            pltpu.VMEM((2, MEMB, BLOCKS, 8, 128), F32),
            pltpu.VMEM((MEMB, BLOCKS, 8, 128), F32),
            pltpu.VMEM((STEPS, 4, 128), F32),
            pltpu.VMEM((STEPS, TILES, 4, 128), F32),
            pltpu.VMEM((8, 128), F32),
            pltpu.VMEM((ENS, 8, 128), F32),
            dma((12,)),
            dma,
            dma,
            dma((STEPS,)),
            dma((STEPS,)),
            dma((STEPS, 2)),
            dma((STEPS, 2)),
            dma,
            dma,
            dma,
        ],
        compiler_params=pltpu.CompilerParams(
            collective_id=0, has_side_effects=True, vmem_limit_bytes=40 * 1024 * 1024
        ),
    )(
        depth, bed, rain, rough_class, class_n.reshape(1, -1), contact_seg, contact_lake,
        lake_slot.reshape(1, -1), storage, area.reshape(1, -1), release.reshape(1, -1),
        upstream_link.reshape(1, -1),
    )
    return water, pool, outflow.reshape(-1)


def solution(mesh):
    return jax.shard_map(
        shards,
        mesh=mesh,
        in_specs=(
            P("ens", "tiles", None),
            P("tiles", None),
            P("ens", "tiles", None),
            P("tiles", None),
            P(),
            P("tiles", None, None),
            P("tiles", None, None),
            P(),
            P("ens", "tiles"),
            P("tiles"),
            P("tiles"),
            P("tiles"),
        ),
        out_specs=(P("ens", "tiles", None), P("ens", "tiles"), P("tiles")),
        check_vma=False,
    )
```

time: 590 us -> 99.7 us (0.17); the launches traced: 582 us -> 99.1 us
  blocking collectives: 179 us -> 0 us
  other arithmetic: 165 us -> 0 us
  Pallas kernels: 0 us -> 84.9 us
  starting transfers between devices: 79.1 us -> 0 us
  local copies, waits for them, and re-layouts: 84.8 us -> 13.5 us
  waiting for transfers between devices: 64.7 us -> 0 us
    all_gather x4 -> x0, blocking collectives: 104 us -> none  [entering(): everything = jax.tree.map(lambda part: lax.all_gather(part, axis), x)]
    scatter-add x4 -> x0, other arithmetic: 91.5 us -> none  [shards(): water = wet_seg.at[:, segments].add(-returned.reshape(members, -1, SEG))....]
    pallas_call x0 -> x1, Pallas kernels: none -> 84.9 us  [shards(): pl.pallas_call(kernel, out_shape=(jax.ShapeDtypeStruct((MEMB, ROWS, COLS)...]
    unnamed x1 -> x0, blocking collectives: 66.1 us -> none
    all_to_all x9 -> x0, starting transfers between devices: 58 us -> none  [the longest x4 32.8 us: shards(): lax.all_to_all(send_rows, 'tiles', split_axis=1, concat_axis=1, tiled=True)]
    all_to_all x9 -> x0, waiting for transfers between devices: 57.1 us -> none  [the longest x4 57.1 us: shards(): lax.all_to_all(send_rows, 'tiles', split_axis=1, concat_axis=1, tiled=True)]
    reshape x17 -> x1, local copies, waits for them, and re-layouts: 47.2 us -> 0.7 us  [shards(): lake_slot.reshape(1, -1)]
    add x12 -> x0, other arithmetic: 23.2 us -> none  [the longest x4 13.8 us: shards(): surface = bed[None] + water]
  transfers between devices with their start and end apart: 17 -> 0, of which waited for: 8 -> 0; matrix products, arithmetic and copies ran while one was open for 6% -> 0% of each run, Pallas kernels for 0% -> 0%
where the time goes in v1:
time: 99.7 us; the launch traced here: 99.1 us
  Pallas kernels  84.9 us (85%)
  local copies, waits for them, and re-layouts  13.5 us (14%)
    pallas_call x1, Pallas kernels, shards(): pl.pallas_call(kernel, out_shape=(jax.ShapeDtypeStruct((MEMB, ROWS, COLS)...  84.9 us
    unnamed x23, local copies, waits for them, and re-layouts  12.8 us

profile of v1, /device:TPU:1, one launch (start us, length us, event | category | flops | bytes accessed | tf_op | source)
XLA Modules:
  0.0 99.1 jit_solution(14318924816645779988)
XLA Ops:
  0.6 0.7 reshape.25.lake_slot
  1.3 0.8 copy.15.contact_seg
  2.1 0.8 copy.16.contact_lake
  2.9 0.0 copy-start
  2.9 1.6 %copy-done = f32[2,16,16384]{2,1,0:T(8,128)S(1)} copy-done((f32[2,16,16384]{2,1,0:T(8,128)S(1)}, f32[2,16,16384]{2,1,0:T(8,128)}, u32[]{:S(2)}) %copy-start) | copy-done | bytes 2097176
  4.4 0.0 copy-start.1
  4.4 1.6 %copy-done.1 = f32[2,16,16384]{2,1,0:T(8,128)S(1)} copy-done((f32[2,16,16384]{2,1,0:T(8,128)S(1)}, f32[2,16,16384]{2,1,0:T(8,128)}, u32[]{:S(2)}) %copy-start.1) | copy-done | bytes 2097176
  6.0 0.0 copy-start.2
  6.0 1.2 %copy-done.2 = f32[16,16384]{1,0:T(8,128)S(1)} copy-done((f32[16,16384]{1,0:T(8,128)S(1)}, f32[16,16384]{1,0:T(8,128)}, u32[]{:S(2)}) %copy-start.2) | copy-done | bytes 1048600
  7.3 0.0 copy-start.3
  7.3 1.2 %copy-done.3 = s32[16,16384]{1,0:T(8,128)S(1)} copy-done((s32[16,16384]{1,0:T(8,128)S(1)}, s32[16,16384]{1,0:T(8,128)}, u32[]{:S(2)}) %copy-start.3) | copy-done | bytes 1048600
  8.5 0.0 copy-start.4
  8.5 0.7 copy-done.4
  9.2 0.0 copy-start.5
  9.2 0.7 copy-done.5
  9.8 0.0 copy-start.6
  9.8 0.7 copy-done.6
  10.5 0.0 copy-start.7
  10.5 0.7 copy-done.7
  11.1 0.0 copy-start.8
  11.1 0.7 copy-done.8
  11.8 84.9 %shard_map.139 = (f32[2,16,16384]{2,1,0:T(8,128)S(1)}, f32[2,40]{1,0:T(2,128)S(1)}, f32[1,40]{1,0:T(1,128)S(1)}) custom-call(f32[2,16,16384]{2,1,0:T(8,128)S(1)} %copy-done, f32[16,16384]{1,0:T(8,128)S(1)} %copy-done.2, f32[2,16,16384]{2,1,0:T(8,128)S(1)} %copy-done.1, s32[16,16384]{1,0:T(8,128)S(1)} %copy-done.3, f32[1,16]{1,0:T(1,128)S(1)} %bitcast.5, ...), custom_call_target="tpu_custom_call" | custom-call | tf_op jit(solution)/shard_map/pallas_call | solution.py:434
  96.7 1.3 %copy.20 = f32[2,16,16384]{2,1,0:T(8,128)} copy(f32[2,16,16384]{2,1,0:T(8,128)S(1)} %get-tuple-element.12) | data formatting | bytes 4194304
  98.0 0.6 copy.21
  98.6 0.5 copy.22
Async XLA Ops:
  2.9 1.6 %copy-start = (f32[2,16,16384]{2,1,0:T(8,128)S(1)}, f32[2,16,16384]{2,1,0:T(8,128)}, u32[]{:S(2)}) copy-start(f32[2,16,16384]{2,1,0:T(8,128)} %depth.1) | copy-start | bytes 6291460
  4.4 1.6 %copy-start.1 = (f32[2,16,16384]{2,1,0:T(8,128)S(1)}, f32[2,16,16384]{2,1,0:T(8,128)}, u32[]{:S(2)}) copy-start(f32[2,16,16384]{2,1,0:T(8,128)} %rain_in.1) | copy-start | bytes 6291460
  6.0 1.2 %copy-start.2 = (f32[16,16384]{1,0:T(8,128)S(1)}, f32[16,16384]{1,0:T(8,128)}, u32[]{:S(2)}) copy-start(f32[16,16384]{1,0:T(8,128)} %bed_in.1) | copy-start | bytes 3145732
  7.3 1.2 %copy-start.3 = (s32[16,16384]{1,0:T(8,128)S(1)}, s32[16,16384]{1,0:T(8,128)}, u32[]{:S(2)}) copy-start(s32[16,16384]{1,0:T(8,128)} %rough.1) | copy-start | bytes 3145732
  8.5 0.7 copy-start.4
  9.2 0.7 copy-start.5
  9.8 0.7 copy-start.6
  10.5 0.7 copy-start.7
  11.1 0.7 copy-start.8

commit v2 on v1

v2 whole, which is shorter than its diff:
```python
import jax
import jax.numpy as jnp
from jax import lax
from jax.experimental import pallas as pl
from jax.experimental.pallas import tpu as pltpu
from jax.sharding import PartitionSpec as P

STEPS = 4
TILES = 32
ENS = 4
MEMB = 2
ROWS = 16
COLS = 16384
BLOCKS = 16
PARTS = 2
CHUNKS = 16
DEPTH = 16
SPAN = BLOCKS // PARTS
LAKE_DEV = 40
FLOW = 0.035
DRAIN = 0.4
FAR = 3.0e38
MESH = pl.DeviceIdType.MESH
F32 = jnp.float32
I32 = jnp.int32


def iota(axis):
    return lax.broadcasted_iota(I32, (8, 128), axis)


def merge(a, b, index, bit, axis):
    odd = (index & bit) != 0
    return jnp.where(odd, b, a) + pltpu.roll(jnp.where(odd, a, b), bit, axis)


def total_of(terms):
    while len(terms) > 1:
        pairs = [terms[n] + terms[n + 1] for n in range(0, len(terms) - 1, 2)]
        terms = pairs + ([terms[-1]] if len(terms) % 2 else [])
    return terms[0]


def spread(row):
    return jnp.broadcast_to(row, (8, 128))


def lanes_of(table, index):
    return jnp.take_along_axis(table, index, axis=1)


def power(water):
    return water * jnp.exp2(jnp.log2(jnp.abs(water)) * (2.0 / 3.0))


def peer_offsets():
    near = {0: 0, 1: 1, 2: 2, 3: 1}
    found = [
        (z, x, c) for z in range(4) for x in range(4) for c in range(2) if (z, x, c) != (0, 0, 0)
    ]
    return sorted(found, key=lambda o: (-near[o[0]] - near[o[1]], o))


def kernel(
    depth, bed_in, rain_in, rough, class_n, contact_seg, contact_lake, lake_slot,
    storage, area, release, link,
    water, new_storage, ens_outflow,
    wat, rain, bed, ivn, wet, rgh,
    seg_s, lake_s, slot_s, cls_v, sto_v, are_v, rel_v, lnk_v,
    hello, greet, turn, pos, pool, outf, par, chain,
    still, still_far, edge, halo, flux, level, part, lines, msg, got, emsg, egot,
    lsem, psem, isem, ssem, rsem, hsend, hrecv, bsend, brecv, esend, erecv,
):
    me = lax.axis_index("tiles")
    ye = lax.axis_index("ens")
    sub, lane = iota(0), iota(1)
    before, after = lax.rem(me + TILES - 1, TILES), lax.rem(me + 1, TILES)
    z, x, core = me // 8, (me // 2) % 4, me % 2
    peers = [
        (lax.rem(z + dz, 4) * 4 + lax.rem(x + dx, 4)) * 2 + lax.rem(core + dc, 2)
        for dz, dx, dc in peer_offsets()
    ]
    others = [lax.rem(ye + k, ENS) for k in range(1, ENS)]

    smalls = [
        (contact_seg, seg_s), (contact_lake, lake_s), (lake_slot, slot_s), (class_n, cls_v),
        (storage, sto_v), (area, are_v), (release, rel_v), (link, lnk_v),
    ]
    bigs = [(rough, rgh), (bed_in, bed), (depth, wat), (rain_in, rain)]
    loads = [pltpu.make_async_copy(a, b, lsem.at[i]) for i, (a, b) in enumerate(smalls + bigs)]
    for load in loads:
        load.start()

    barrier = pltpu.get_barrier_semaphore()
    for peer in peers:
        pl.semaphore_signal(barrier, inc=1, device_id={"tiles": peer}, device_id_type=MESH)
    for other in others:
        pl.semaphore_signal(barrier, inc=1, device_id={"ens": other}, device_id_type=MESH)

    for load in loads[: len(smalls)]:
        load.wait()

    seg_id = ((lane & 1) * 8 + sub) * 64 + (lane >> 1)
    contact_id = (lane & 31) * 8 + sub * 4 + (lane >> 5)

    def read_contacts(e, carry):
        code, from_seg, where_to = carry
        for c in range(8):
            seg = seg_s[0, c, e]
            lake = lake_s[0, c, e]
            live = lake >= 0
            place = slot_s[jnp.maximum(lake, 0)] - e * LAKE_DEV
            code = jnp.where(seg_id == seg, jnp.where(live, place * 32 + e, -1), code)
            mine = (contact_id == e * 8 + c) & (sub < 2)
            from_seg = jnp.where(mine, seg, from_seg)
            where_to = jnp.where(mine, jnp.where(live, place, -1), where_to)
        return code, from_seg, where_to

    none = jnp.full((8, 128), -1, I32)
    code, from_seg, where_to = lax.fori_loop(
        0, TILES, read_contacts, (none, jnp.zeros((8, 128), I32), none)
    )
    code_row, code_lane = code >> 7, code & 127
    src_sub = (from_seg >> 6) & 7
    src_lane = (from_seg & 63) * 2 + (from_seg >> 9)

    hello[...] = jnp.zeros((8, 128), F32)
    hello[0:2, :] = where_to.astype(F32)[0:2, :]
    hello[2:4, 0:LAKE_DEV] = sto_v[...]
    hello[4:5, 0:LAKE_DEV] = are_v[...]
    hello[5:6, 0:LAKE_DEV] = rel_v[...]
    hello[6:7, 0:LAKE_DEV] = lnk_v[...].astype(F32)

    pl.semaphore_wait(barrier, TILES - 1 + ENS - 1)
    for peer in peers:
        pltpu.make_async_remote_copy(
            hello, greet.at[me], psem, isem, device_id={"tiles": peer}, device_id_type=MESH
        ).start()
    pltpu.make_async_copy(hello, greet.at[me], isem).start()

    for load in loads[len(smalls):]:
        load.wait()
    inverse = (0.5 * FLOW) / cls_v[...]
    classes = [spread(inverse[:, n:n + 1]) for n in range(16)]

    def inverse_of(index):
        found = classes
        for bit in (1, 2, 4, 8):
            odd = (index & bit) != 0
            found = [jnp.where(odd, found[n + 1], found[n]) for n in range(0, len(found), 2)]
        return found[0]

    def read_rough(i, carry):
        base = pl.multiple_of(i * 1024, 1024)
        for j in range(8):
            cols = pl.ds(base + j * 128, 128)
            for half in range(2):
                rows = slice(half * 8, half * 8 + 8)
                ivn[rows, cols] = inverse_of(rgh[rows, cols])
            for side, row in ((0, 0), (1, 15)):
                edge[0, side, 0, i, j:j + 1, :] = wat[0, row:row + 1, cols]
                edge[0, side, 1, i, j:j + 1, :] = wat[1, row:row + 1, cols]
                still[side, 0, i, j:j + 1, :] = bed[row:row + 1, cols]
                still[side, 1, i, j:j + 1, :] = ivn[row:row + 1, cols]
        return carry

    lax.fori_loop(0, BLOCKS, read_rough, 0)

    def beside(side):
        return {"tiles": (before, after)[side]}

    still_copies = [
        pltpu.make_async_remote_copy(
            still.at[side], still_far.at[1 - side], bsend.at[side], brecv.at[side],
            device_id=beside(side), device_id_type=MESH,
        )
        for side in (0, 1)
    ]

    def halo_copies(step, p):
        at = pl.ds(p * SPAN, SPAN)
        return [
            pltpu.make_async_remote_copy(
                edge.at[step, side, :, at], halo.at[step, 1 - side, :, at],
                hsend.at[step, side, p], hrecv.at[step, side, p],
                device_id=beside(side), device_id_type=MESH,
            )
            for side in (0, 1)
        ]

    def edge_flows(step):
        inside = (me > 0, me < TILES - 1)

        def edge_flux(i, carry):
            for side in (0, 1):
                for m in range(MEMB):
                    w_own, w_far = edge[step, side, m, i], halo[step, side, m, i]
                    s_own, s_far = w_own + still[side, 0, i], w_far + still_far[side, 0, i]
                    m_own = power(w_own) * still[side, 1, i]
                    m_far = power(w_far) * still_far[side, 1, i]
                    flux[side, m, i] = jnp.where(
                        inside[side], (m_own + m_far) * (s_far - s_own), 0.0
                    )
            return carry

        for p in range(PARTS):
            for copy in halo_copies(step, p):
                copy.wait_recv()
        lax.fori_loop(0, BLOCKS, edge_flux, 0, unroll=2)

    def flows(step, m):
        top, bottom = sub == 0, sub == 7
        first, last = lane == 0, lane == 127

        def block(i, carry):
            carry = list(carry)
            base = pl.multiple_of(i * (128 * CHUNKS), 128 * CHUNKS)
            for j in range(CHUNKS):
                cols = pl.ds(base + j * 128, 128)
                w = [wat[m, h * 8:h * 8 + 8, cols] for h in range(2)]
                s = [bed[h * 8:h * 8 + 8, cols] + w[h] for h in range(2)]
                mo = [power(w[h]) * ivn[h * 8:h * 8 + 8, cols] for h in range(2)]
                s_dn = [pltpu.roll(v, 1, 0) for v in s]
                m_dn = [pltpu.roll(v, 1, 0) for v in mo]
                fv0 = jnp.where(top, 0.0, (m_dn[0] + mo[0]) * (s_dn[0] - s[0]))
                fv1 = (jnp.where(top, m_dn[0], m_dn[1]) + mo[1]) * (
                    jnp.where(top, s_dn[0], s_dn[1]) - s[1]
                )
                up0, up1 = pltpu.roll(fv0, 7, 0), pltpu.roll(fv1, 7, 0)
                nv = [
                    fv0 - jnp.where(bottom, up1, up0),
                    fv1 - jnp.where(bottom, 0.0, up1),
                ]
                for h in range(2):
                    s_prev, m_prev, f_prev, sum_prev = carry[h * 4:h * 4 + 4]
                    s_rt, m_rt = pltpu.roll(s[h], 1, 1), pltpu.roll(mo[h], 1, 1)
                    f = (jnp.where(first, m_prev, m_rt) + mo[h]) * (
                        jnp.where(first, s_prev, s_rt) - s[h]
                    )
                    f_lt = pltpu.roll(f, 127, 1)
                    wet[m, h * 8:h * 8 + 8, cols] = sum_prev - jnp.where(last, f_lt, f_prev)
                    total = (w[h] + rain[m, h * 8:h * 8 + 8, cols]) + (nv[h] + f)
                    carry[h * 4:h * 4 + 4] = [s_rt, m_rt, f_lt, total]
            return tuple(carry)

        zero = jnp.zeros((8, 128), F32)
        start = []
        for h in range(2):
            rows = slice(h * 8, h * 8 + 8)
            start += [bed[rows, 0:128] + wat[m, rows, 0:128], zero, zero, zero]
        carry = lax.fori_loop(0, COLS // 128 // CHUNKS, block, tuple(start))
        for h in range(2):
            f_prev, sum_prev = carry[h * 4 + 2:h * 4 + 4]
            wet[m, h * 8:h * 8 + 8, COLS:COLS + 128] = sum_prev - jnp.where(last, 0.0, f_prev)

    def drain(step):
        found = []
        for m in range(MEMB):
            now = [pool[m, v] * par[0, v] for v in range(2)]
            value = jnp.full((8, 128), FAR, F32)
            for j in range(LAKE_DEV // 4):
                row = spread(now[j // 8][j % 8:j % 8 + 1, :])
                value = jnp.where(code_row == j, lanes_of(row, code_lane), value)
            found.append(value)

        def set_levels(i, turned):
            for n in range(8):
                for m in range(MEMB):
                    level[m, i, n] = spread(turned[m][:, n:n + 1])
            return [pltpu.roll(value, 120, 1) for value in turned]

        def block(i, turned):
            turned = set_levels(i + 1, turned)
            base = pl.multiple_of(i * 1024, 1024)
            for g in range(4):
                for m in range(MEMB):
                    for h in range(2):
                        rows = slice(h * 8, h * 8 + 8)
                        low = level[m, i, 2 * g + h]
                        leaf = None
                        for j in (2 * g, 2 * g + 1):
                            cols = pl.ds(base + j * 128, 128)
                            w = wet[m, rows, pl.ds(base + j * 128 + 128, 128)]
                            over = spread(flux[h, m, i, j:j + 1, :])
                            w = w + jnp.where(sub == 7 * h, over, 0.0)
                            excess = jnp.maximum((bed[rows, cols] + w) - low, 0.0)
                            taken = (DRAIN * w) * (excess / (1.0 + excess))
                            left = w - taken
                            if step < STEPS - 1:
                                wat[m, rows, cols] = left
                                r = 0 if h == 0 else 7
                                edge[step + 1, h, m, i, j:j + 1, :] = left[r:r + 1, :]
                            else:
                                water[m, rows, cols] = left
                            leaf = taken if leaf is None else leaf + taken
                        part[m, i, 2 * g + h] = leaf
            return tuple(turned)

        turned = tuple(set_levels(0, found))
        for p in range(PARTS):
            turned = lax.fori_loop(p * SPAN, p * SPAN + SPAN, block, turned)
            if step < STEPS - 1:
                for copy in halo_copies(step + 1, p):
                    copy.start()
        sums = []
        for m in range(MEMB):
            groups = []
            for i in range(BLOCKS):
                leaves = [part[m, i, n] for n in range(8)]
                for bit in (1, 2, 4):
                    leaves = [
                        merge(leaves[n], leaves[n + 1], lane, bit, 1)
                        for n in range(0, len(leaves), 2)
                    ]
                groups.append(leaves[0])
            for bit in (8, 16, 32, 64):
                groups = [
                    merge(groups[n], groups[n + 1], lane, bit, 1) for n in range(0, len(groups), 2)
                ]
            sums.append(groups[0])
        return sums

    def tell(step, sums):
        picked = [jnp.zeros((8, 128), F32) for _ in range(MEMB)]
        for k in range(8):
            here = src_sub == k
            for m in range(MEMB):
                row = spread(sums[m][k:k + 1, :])
                picked[m] = jnp.where(here, lanes_of(row, src_lane), picked[m])
        for m in range(MEMB):
            msg[step, m] = picked[m][0:2, :]
        for peer in peers:
            pltpu.make_async_remote_copy(
                msg.at[step], got.at[step, me], ssem.at[step], rsem.at[step],
                device_id={"tiles": peer}, device_id_type=MESH,
            ).start()
        pltpu.make_async_copy(msg.at[step], got.at[step, me], rsem.at[step]).start()

    def hear(step):
        pltpu.make_async_copy(got.at[step], got.at[step], rsem.at[step]).wait()
        places = [pos[n] for n in range(TILES // 4)]
        for m in range(MEMB):
            values = [
                jnp.concatenate([got[step, 4 * n + d, m] for d in range(4)], axis=0)
                for n in range(TILES // 4)
            ]
            for j in range(LAKE_DEV // 4):
                leaves = []
                for p in range(4 * j, 4 * j + 4):
                    terms = [
                        jnp.where(places[n] == float(p), values[n], 0.0) for n in range(TILES // 4)
                    ]
                    leaves.append(total_of(terms))
                for bit in (32, 64):
                    leaves = [
                        merge(leaves[n], leaves[n + 1], lane, bit, 1)
                        for n in range(0, len(leaves), 2)
                    ]
                lines[m, j * 8:j * 8 + 8, :] = leaves[0]
        for m in range(MEMB):
            for v in range(2):
                lateral = total_of([lines[m, pl.ds(v * 64 + r, 8, stride=8), :] for r in range(8)])
                full = pool[m, v] + lateral * (1.0 / 256.0)
                out = par[1, v] * full
                above = total_of(
                    [chain[k, v] * pltpu.roll(out, k + 1, 1) for k in range(DEPTH - 1)]
                )
                out = out + par[1, v] * above
                pool[m, v] = full + above - out
                outf[m, v] = outf[m, v] + out

    for side in (0, 1):
        still_copies[side].start()
    for p in range(PARTS):
        for copy in halo_copies(0, p):
            copy.start()
    for m in range(MEMB):
        flows(0, m)

    pltpu.make_async_copy(greet, greet, isem).wait()
    for n in range(TILES // 4):
        pos[n] = jnp.concatenate([greet[4 * n + d, 0:2, :] for d in range(4)], axis=0)
    for k in range(4):
        pick = (lane & 15) * 4 + k
        for b in range(4):
            tile = jnp.zeros((8, 128), F32)
            for kind in range(5):
                rows = greet[b * 8:b * 8 + 8, 2 + kind, :]
                tile = jnp.where((lane >> 4) == kind, lanes_of(rows, pick), tile)
            turn[k * 32 + b * 8:k * 32 + b * 8 + 8, :] = tile
    turn[...] = jnp.transpose(turn[...])
    for v in range(2):
        used = sub + 8 * v < LAKE_DEV // 4
        rows = [turn[16 * kind + 8 * v:16 * kind + 8 * v + 8, :] for kind in range(5)]
        for m in range(MEMB):
            pool[m, v] = rows[m]
            outf[m, v] = jnp.zeros((8, 128), F32)
            lines[m, 64 + 8 * v:72 + 8 * v, :] = jnp.zeros((8, 128), F32)
            lines[m, 80 + 24 * v:104 + 24 * v, :] = jnp.zeros((24, 128), F32)
        par[0, v] = 1.0 / jnp.where(used, rows[2], 1.0)
        par[1, v] = rows[3]
        share = rows[3] * rows[4]
        run = rows[4]
        for k in range(DEPTH - 1):
            chain[k, v] = run
            run = run * pltpu.roll(share, k + 1, 1)

    for copy in still_copies:
        copy.wait_recv()
    for step in range(STEPS):
        edge_flows(step)
        if step > 0:
            hear(step - 1)
        sums = drain(step)
        tell(step, sums)
        if step < STEPS - 1:
            for m in range(MEMB):
                flows(step + 1, m)
    hear(STEPS - 1)

    pick = (lane & 3) * 32 + me
    own = [jnp.zeros((8, 128), F32) for _ in range(2)]
    for m in range(MEMB):
        for j in range(LAKE_DEV // 4):
            here = (lane >> 2) == j
            v, r = j // 8, j % 8
            own[0] = jnp.where(
                here & (sub == m), lanes_of(spread(pool[m, v, r:r + 1, :]), pick), own[0]
            )
            own[1] = own[1] + jnp.where(here, lanes_of(spread(outf[m, v, r:r + 1, :]), pick), 0.0)
    emsg[...] = own[1]
    for other in others:
        pltpu.make_async_remote_copy(
            emsg, egot.at[ye], esend, erecv, device_id={"ens": other}, device_id_type=MESH
        ).start()
    pltpu.make_async_copy(emsg, egot.at[ye], erecv).start()
    new_storage[...] = own[0][0:2, 0:LAKE_DEV]
    pltpu.make_async_copy(greet.at[1:], greet.at[1:], psem).wait()
    for copy in still_copies:
        copy.wait_send()
    for step in range(STEPS):
        for p in range(PARTS):
            for copy in halo_copies(step, p):
                copy.wait_send()
        pltpu.make_async_copy(got.at[step, 1:], got.at[step, 1:], ssem.at[step]).wait()
    pltpu.make_async_copy(egot, egot, erecv).wait()
    total = (egot[0] + egot[1] + egot[2] + egot[3]) * (1.0 / (MEMB * ENS))
    ens_outflow[...] = total[0:1, 0:LAKE_DEV]
    pltpu.make_async_copy(egot.at[1:], egot.at[1:], esend).wait()


def hand_out(water, pool, outflow, new_depth, new_storage, ens_outflow, sem):
    copies = [
        pltpu.make_async_copy(a, b, sem.at[n])
        for n, (a, b) in enumerate(
            [
                (water.at[0], new_depth.at[0]), (water.at[1], new_depth.at[1]),
                (pool, new_storage), (outflow, ens_outflow),
            ]
        )
    ]
    for copy in copies:
        copy.start()
    for copy in copies:
        copy.wait()


def shards(
    depth, bed, rain, rough_class, class_n, contact_seg, contact_lake, lake_slot,
    storage, area, release, upstream_link,
):
    far = pl.BlockSpec(memory_space=pltpu.HBM)
    vmem = pl.BlockSpec(memory_space=pltpu.VMEM)
    dma = pltpu.SemaphoreType.DMA
    results = pl.pallas_call(
        kernel,
        out_shape=(
            jax.ShapeDtypeStruct((MEMB, ROWS, COLS), F32),
            jax.ShapeDtypeStruct((MEMB, LAKE_DEV), F32),
            jax.ShapeDtypeStruct((1, LAKE_DEV), F32),
        ),
        in_specs=[far] * 12,
        out_specs=(vmem, vmem, vmem),
        scratch_shapes=[
            pltpu.VMEM((MEMB, ROWS, COLS), F32),
            pltpu.VMEM((MEMB, ROWS, COLS), F32),
            pltpu.VMEM((ROWS, COLS), F32),
            pltpu.VMEM((ROWS, COLS), F32),
            pltpu.VMEM((MEMB, ROWS, COLS + 128), F32),
            pltpu.VMEM((ROWS, COLS), I32),
            pltpu.SMEM((1, 8, TILES), I32),
            pltpu.SMEM((1, 8, TILES), I32),
            pltpu.SMEM((TILES * LAKE_DEV,), I32),
            pltpu.VMEM((1, 16), F32),
            pltpu.VMEM((MEMB, LAKE_DEV), F32),
            pltpu.VMEM((1, LAKE_DEV), F32),
            pltpu.VMEM((1, LAKE_DEV), F32),
            pltpu.VMEM((1, LAKE_DEV), I32),
            pltpu.VMEM((8, 128), F32),
            pltpu.VMEM((TILES, 8, 128), F32),
            pltpu.VMEM((128, 128), F32),
            pltpu.VMEM((TILES // 4, 8, 128), F32),
            pltpu.VMEM((MEMB, 2, 8, 128), F32),
            pltpu.VMEM((MEMB, 2, 8, 128), F32),
            pltpu.VMEM((2, 2, 8, 128), F32),
            pltpu.VMEM((DEPTH - 1, 2, 8, 128), F32),
            pltpu.VMEM((2, 2, BLOCKS, 8, 128), F32),
            pltpu.VMEM((2, 2, BLOCKS, 8, 128), F32),
            pltpu.VMEM((STEPS, 2, MEMB, BLOCKS, 8, 128), F32),
            pltpu.VMEM((STEPS, 2, MEMB, BLOCKS, 8, 128), F32),
            pltpu.VMEM((2, MEMB, BLOCKS, 8, 128), F32),
            pltpu.VMEM((MEMB, BLOCKS + 1, 8, 8, 128), F32),
            pltpu.VMEM((MEMB, BLOCKS, 8, 8, 128), F32),
            pltpu.VMEM((MEMB, 128, 128), F32),
            pltpu.VMEM((STEPS, MEMB, 2, 128), F32),
            pltpu.VMEM((STEPS, TILES, MEMB, 2, 128), F32),
            pltpu.VMEM((8, 128), F32),
            pltpu.VMEM((ENS, 8, 128), F32),
            dma((12,)),
            dma,
            dma,
            dma((STEPS,)),
            dma((STEPS,)),
            dma((STEPS, 2, PARTS)),
            dma((STEPS, 2, PARTS)),
            dma((2,)),
            dma((2,)),
            dma,
            dma,
        ],
        compiler_params=pltpu.CompilerParams(
            collective_id=0, has_side_effects=True, vmem_limit_bytes=40 * 1024 * 1024
        ),
    )(
        *[
            pltpu.with_memory_space_constraint(a, pltpu.HBM)
            for a in (
                depth, bed, rain, rough_class, class_n.reshape(1, -1),
                contact_seg.transpose(0, 2, 1), contact_lake.transpose(0, 2, 1),
                lake_slot, storage, area.reshape(1, -1), release.reshape(1, -1),
                upstream_link.reshape(1, -1),
            )
        ]
    )
    water, pool, outflow = pl.pallas_call(
        hand_out,
        out_shape=[jax.ShapeDtypeStruct(r.shape, r.dtype) for r in results],
        in_specs=[vmem] * 3,
        out_specs=(far, far, far),
        scratch_shapes=[dma((4,))],
        compiler_params=pltpu.CompilerParams(vmem_limit_bytes=1024 * 1024),
    )(*results)
    return water, pool, outflow.reshape(-1)


def solution(mesh):
    return jax.shard_map(
        shards,
        mesh=mesh,
        in_specs=(
            P("ens", "tiles", None),
            P("tiles", None),
            P("ens", "tiles", None),
            P("tiles", None),
            P(),
            P("tiles", None, None),
            P("tiles", None, None),
            P(),
            P("ens", "tiles"),
            P("tiles"),
            P("tiles"),
            P("tiles"),
        ),
        out_specs=(P("ens", "tiles", None), P("ens", "tiles"), P("tiles")),
        check_vma=False,
    )
```

time: 99.7 us -> 53 us (0.53)
  Pallas kernels: 84.9 us -> 52.2 us
  local copies, waits for them, and re-layouts: 13.5 us -> 0 us
    pallas_call x1, Pallas kernels: 84.9 us -> 50.9 us  [shards(): pl.pallas_call(kernel, out_shape=(jax.ShapeDtypeStruct((MEMB, ROWS, COLS)...]
    unnamed x23 -> x0, local copies, waits for them, and re-layouts: 12.8 us -> none
    pallas_call x0 -> x1, Pallas kernels: none -> 1.36 us  [shards(): pl.pallas_call(hand_out, out_shape=[jax.ShapeDtypeStruct(r.shape, r.dtype...]
where the time goes in v2:
time: 53 us; the launch traced here: 52.9 us
  Pallas kernels  52.2 us (98%)
  between operations  0.64 us (1%)
    pallas_call x1, Pallas kernels, shards(): pl.pallas_call(kernel, out_shape=(jax.ShapeDtypeStruct((MEMB, ROWS, COLS)...  50.9 us
    pallas_call x1, Pallas kernels, shards(): pl.pallas_call(hand_out, out_shape=[jax.ShapeDtypeStruct(r.shape, r.dtype...  1.36 us

profile of v2, /device:TPU:1, one launch (start us, length us, event | category | flops | bytes accessed | tf_op | source)
XLA Modules:
  0.0 52.9 jit_solution(11023713433533701824)
XLA Ops:
  0.6 50.9 %shard_map.139 = (f32[2,16,16384]{2,1,0:T(8,128)S(1)}, f32[2,40]{1,0:T(2,128)S(1)}, f32[1,40]{1,0:T(1,128)S(1)}) custom-call(f32[2,16,16384]{2,1,0:T(8,128)} %depth.1, f32[16,16384]{1,0:T(8,128)} %bed_in.1, f32[2,16,16384]{2,1,0:T(8,128)} %rain_in.1, s32[16,16384]{1,0:T(8,128)} %rough.1, f32[1,16]{1,0:T(1,128)} %bitcast.9, s32[1,8,32]{2,1,0:T(8,128)} %bitcast.7, ...), custom_call_target="tpu_custom_call" | custom-call | tf_op jit(solution)/shard_map/pallas_call | solution.py:475
  51.5 1.4 %shard_map.140 = (f32[2,16,16384]{2,1,0:T(8,128)}, f32[2,40]{1,0:T(2,128)}, f32[1,40]{1,0:T(1,128)}) custom-call(f32[2,16,16384]{2,1,0:T(8,128)S(1)} %get-tuple-element.9.water, f32[2,40]{1,0:T(2,128)S(1)} %get-tuple-element.10.pool, f32[1,40]{1,0:T(1,128)S(1)} %get-tuple-element.11.outflow), custom_call_target="tpu_custom_call" | custom-call | tf_op jit(solution)/shard_map/pallas_call | solution.py:545

commit v3 on v2

--- a/solution.py
+++ b/solution.py
@@ -68,8 +68,8 @@
     wat, rain, bed, ivn, wet, rgh,
     seg_s, lake_s, slot_s, cls_v, sto_v, are_v, rel_v, lnk_v,
     hello, greet, turn, pos, pool, outf, par, chain,
-    still, still_far, edge, halo, flux, level, part, lines, msg, got, emsg, egot,
-    lsem, psem, isem, ssem, rsem, hsend, hrecv, bsend, brecv, esend, erecv,
+    still, still_far, edge, halo, flux, level, part, lines, msg, got, emsg, egot, share, shared,
+    lsem, psem, isem, ssem, rsem, hsend, hrecv, bsend, brecv, esend, erecv, psend, precv, all_in,
 ):
     me = lax.axis_index("tiles")
     ye = lax.axis_index("ens")
@@ -81,6 +81,7 @@
         for dz, dx, dc in peer_offsets()
     ]
     others = [lax.rem(ye + k, ENS) for k in range(1, ENS)]
+    strangers = [{"tiles": peer, "ens": others[k]} for k in (1, 0, 2) for peer in peers + [me]]
 
     smalls = [
         (contact_seg, seg_s), (contact_lake, lake_s), (lake_slot, slot_s), (class_n, cls_v),
@@ -130,13 +131,6 @@
     hello[4:5, 0:LAKE_DEV] = are_v[...]
     hello[5:6, 0:LAKE_DEV] = rel_v[...]
     hello[6:7, 0:LAKE_DEV] = lnk_v[...].astype(F32)
-
-    pl.semaphore_wait(barrier, TILES - 1 + ENS - 1)
-    for peer in peers:
-        pltpu.make_async_remote_copy(
-            hello, greet.at[me], psem, isem, device_id={"tiles": peer}, device_id_type=MESH
-        ).start()
-    pltpu.make_async_copy(hello, greet.at[me], isem).start()
 
     for load in loads[len(smalls):]:
         load.wait()
@@ -164,6 +158,15 @@
                 still[side, 1, i, j:j + 1, :] = ivn[row:row + 1, cols]
         return carry
 
+
+    pl.semaphore_wait(barrier, TILES - 1 + ENS - 1)
+    for other in others:
+        pl.semaphore_signal(all_in, inc=1, device_id={"ens": other}, device_id_type=MESH)
+    for peer in peers:
+        pltpu.make_async_remote_copy(
+            hello, greet.at[me], psem, isem, device_id={"tiles": peer}, device_id_type=MESH
+        ).start()
+    pltpu.make_async_copy(hello, greet.at[me], isem).start()
     lax.fori_loop(0, BLOCKS, read_rough, 0)
 
     def beside(side):
@@ -298,7 +301,7 @@
 
         turned = tuple(set_levels(0, found))
         for p in range(PARTS):
-            turned = lax.fori_loop(p * SPAN, p * SPAN + SPAN, block, turned)
+            turned = lax.fori_loop(p * SPAN, p * SPAN + SPAN, block, turned, unroll=2)
             if step < STEPS - 1:
                 for copy in halo_copies(step + 1, p):
                     copy.start()
@@ -335,39 +338,73 @@
                 device_id={"tiles": peer}, device_id_type=MESH,
             ).start()
         pltpu.make_async_copy(msg.at[step], got.at[step, me], rsem.at[step]).start()
-
-    def hear(step):
+        if step == STEPS - 1:
+            emsg[...] = (picked[0] + picked[1])[0:2, :]
+            pl.semaphore_wait(all_in, ENS - 1)
+            for stranger in strangers:
+                pltpu.make_async_remote_copy(
+                    emsg, egot.at[ye, me], esend, erecv, device_id=stranger, device_id_type=MESH
+                ).start()
+
+    places = []
+
+    def slot_sums(values, m):
+        for j in range(LAKE_DEV // 4):
+            leaves = [
+                total_of([jnp.where(at == float(p), v, 0.0) for at, v in zip(places, values)])
+                for p in range(4 * j, 4 * j + 4)
+            ]
+            for bit in (32, 64):
+                leaves = [
+                    merge(leaves[n], leaves[n + 1], lane, bit, 1) for n in range(0, len(leaves), 2)
+                ]
+            lines[m, j * 8:j * 8 + 8, :] = leaves[0]
+
+    def cascade(held, m, v):
+        lateral = total_of([lines[m, pl.ds(v * 64 + r, 8, stride=8), :] for r in range(8)])
+        full = held + lateral * (1.0 / 256.0)
+        out = par[1, v] * full
+        above = total_of([chain[k, v] * pltpu.roll(out, k + 1, 1) for k in range(DEPTH - 1)])
+        out = out + par[1, v] * above
+        return full + above - out, out
+
+    def heard(step):
         pltpu.make_async_copy(got.at[step], got.at[step], rsem.at[step]).wait()
-        places = [pos[n] for n in range(TILES // 4)]
-        for m in range(MEMB):
-            values = [
+        places[:] = [pos[n] for n in range(TILES // 4)]
+        return [
+            [
                 jnp.concatenate([got[step, 4 * n + d, m] for d in range(4)], axis=0)
                 for n in range(TILES // 4)
             ]
-            for j in range(LAKE_DEV // 4):
-                leaves = []
-                for p in range(4 * j, 4 * j + 4):
-                    terms = [
-                        jnp.where(places[n] == float(p), values[n], 0.0) for n in range(TILES // 4)
-                    ]
-                    leaves.append(total_of(terms))
-                for bit in (32, 64):
-                    leaves = [
-                        merge(leaves[n], leaves[n + 1], lane, bit, 1)
-                        for n in range(0, len(leaves), 2)
-                    ]
-                lines[m, j * 8:j * 8 + 8, :] = leaves[0]
+            for m in range(MEMB)
+        ]
+
+    def hear(step):
+        values = heard(step)
+        for m in range(MEMB):
+            slot_sums(values[m], m)
         for m in range(MEMB):
             for v in range(2):
-                lateral = total_of([lines[m, pl.ds(v * 64 + r, 8, stride=8), :] for r in range(8)])
-                full = pool[m, v] + lateral * (1.0 / 256.0)
-                out = par[1, v] * full
-                above = total_of(
-                    [chain[k, v] * pltpu.roll(out, k + 1, 1) for k in range(DEPTH - 1)]
-                )
-                out = out + par[1, v] * above
-                pool[m, v] = full + above - out
-                outf[m, v] = outf[m, v] + out
+                pool[m, v], out = cascade(pool[m, v], m, v)
+                if step < STEPS - 1:
+                    outf[m, v] = outf[m, v] + out
+        return values
+
+    def share_copies():
+        return [
+            pltpu.make_async_remote_copy(
+                share, shared.at[ye], psend, precv, device_id={"ens": other}, device_id_type=MESH
+            )
+            for other in others
+        ]
+
+    def share_start():
+        for v in range(2):
+            share[0, v] = pool[0, v] + pool[1, v]
+            share[1, v] = outf[0, v] + outf[1, v]
+        for copy in share_copies():
+            copy.start()
+        pltpu.make_async_copy(share, shared.at[ye], precv).start()
 
     for side in (0, 1):
         still_copies[side].start()
@@ -389,21 +426,21 @@
                 tile = jnp.where((lane >> 4) == kind, lanes_of(rows, pick), tile)
             turn[k * 32 + b * 8:k * 32 + b * 8 + 8, :] = tile
     turn[...] = jnp.transpose(turn[...])
+    for m in range(MEMB + 1):
+        lines[m, 80:128, :] = jnp.zeros((48, 128), F32)
     for v in range(2):
         used = sub + 8 * v < LAKE_DEV // 4
         rows = [turn[16 * kind + 8 * v:16 * kind + 8 * v + 8, :] for kind in range(5)]
         for m in range(MEMB):
             pool[m, v] = rows[m]
             outf[m, v] = jnp.zeros((8, 128), F32)
-            lines[m, 64 + 8 * v:72 + 8 * v, :] = jnp.zeros((8, 128), F32)
-            lines[m, 80 + 24 * v:104 + 24 * v, :] = jnp.zeros((24, 128), F32)
         par[0, v] = 1.0 / jnp.where(used, rows[2], 1.0)
         par[1, v] = rows[3]
-        share = rows[3] * rows[4]
+        factor = rows[3] * rows[4]
         run = rows[4]
         for k in range(DEPTH - 1):
             chain[k, v] = run
-            run = run * pltpu.roll(share, k + 1, 1)
+            run = run * pltpu.roll(factor, k + 1, 1)
 
     for copy in still_copies:
         copy.wait_recv()
@@ -413,28 +450,49 @@
             hear(step - 1)
         sums = drain(step)
         tell(step, sums)
-        if step < STEPS - 1:
+        if step == STEPS - 1:
+            share_start()
+        else:
             for m in range(MEMB):
                 flows(step + 1, m)
-    hear(STEPS - 1)
+    values = hear(STEPS - 1)
+
+    pltpu.make_async_copy(shared, shared, precv).wait()
+    pltpu.make_async_copy(egot.at[1:], egot.at[1:], erecv).wait()
+    everyone = []
+    for n in range(TILES // 4):
+        mine = values[0][n] + values[1][n]
+        everyone.append(
+            total_of(
+                [
+                    jnp.where(
+                        ye == y,
+                        mine,
+                        jnp.concatenate([egot[y, 4 * n + d] for d in range(4)], axis=0),
+                    )
+                    for y in range(ENS)
+                ]
+            )
+        )
+    slot_sums(everyone, MEMB)
+    sum_of = [
+        [total_of([shared[y, kind, v] for y in range(ENS)]) for v in range(2)] for kind in range(2)
+    ]
+    outflow = [sum_of[1][v] + cascade(sum_of[0][v], MEMB, v)[1] for v in range(2)]
 
     pick = (lane & 3) * 32 + me
     own = [jnp.zeros((8, 128), F32) for _ in range(2)]
-    for m in range(MEMB):
-        for j in range(LAKE_DEV // 4):
-            here = (lane >> 2) == j
-            v, r = j // 8, j % 8
+    for j in range(LAKE_DEV // 4):
+        here = (lane >> 2) == j
+        v, r = j // 8, j % 8
+        for m in range(MEMB):
             own[0] = jnp.where(
                 here & (sub == m), lanes_of(spread(pool[m, v, r:r + 1, :]), pick), own[0]
             )
-            own[1] = own[1] + jnp.where(here, lanes_of(spread(outf[m, v, r:r + 1, :]), pick), 0.0)
-    emsg[...] = own[1]
-    for other in others:
-        pltpu.make_async_remote_copy(
-            emsg, egot.at[ye], esend, erecv, device_id={"ens": other}, device_id_type=MESH
-        ).start()
-    pltpu.make_async_copy(emsg, egot.at[ye], erecv).start()
+        own[1] = jnp.where(here, lanes_of(spread(outflow[v][r:r + 1, :]), pick), own[1])
     new_storage[...] = own[0][0:2, 0:LAKE_DEV]
+    ens_outflow[...] = (own[1] * (1.0 / (MEMB * ENS)))[0:1, 0:LAKE_DEV]
+
     pltpu.make_async_copy(greet.at[1:], greet.at[1:], psem).wait()
     for copy in still_copies:
         copy.wait_send()
@@ -443,9 +501,7 @@
             for copy in halo_copies(step, p):
                 copy.wait_send()
         pltpu.make_async_copy(got.at[step, 1:], got.at[step, 1:], ssem.at[step]).wait()
-    pltpu.make_async_copy(egot, egot, erecv).wait()
-    total = (egot[0] + egot[1] + egot[2] + egot[3]) * (1.0 / (MEMB * ENS))
-    ens_outflow[...] = total[0:1, 0:LAKE_DEV]
+    pltpu.make_async_copy(shared.at[1:], shared.at[1:], psend).wait()
     pltpu.make_async_copy(egot.at[1:], egot.at[1:], esend).wait()
 
 
@@ -511,11 +567,13 @@
             pltpu.VMEM((2, MEMB, BLOCKS, 8, 128), F32),
             pltpu.VMEM((MEMB, BLOCKS + 1, 8, 8, 128), F32),
             pltpu.VMEM((MEMB, BLOCKS, 8, 8, 128), F32),
-            pltpu.VMEM((MEMB, 128, 128), F32),
+            pltpu.VMEM((MEMB + 1, 128, 128), F32),
             pltpu.VMEM((STEPS, MEMB, 2, 128), F32),
             pltpu.VMEM((STEPS, TILES, MEMB, 2, 128), F32),
-            pltpu.VMEM((8, 128), F32),
-            pltpu.VMEM((ENS, 8, 128), F32),
+            pltpu.VMEM((2, 128), F32),
+            pltpu.VMEM((ENS, TILES, 2, 128), F32),
+            pltpu.VMEM((2, 2, 8, 128), F32),
+            pltpu.VMEM((ENS, 2, 2, 8, 128), F32),
             dma((12,)),
             dma,
             dma,
@@ -527,6 +585,9 @@
             dma((2,)),
             dma,
             dma,
+            dma,
+            dma,
+            pltpu.SemaphoreType.REGULAR,
         ],
         compiler_params=pltpu.CompilerParams(
             collective_id=0, has_side_effects=True, vmem_limit_bytes=40 * 1024 * 1024

time: 53 us -> 51.8 us (0.977)
  Pallas kernels: 52.2 us -> 51 us
    pallas_call x1, Pallas kernels: 50.9 us -> 49.7 us  [shards(): pl.pallas_call(kernel, out_shape=(jax.ShapeDtypeStruct((MEMB, ROWS, COLS)...]
where the time goes in v3:
time: 51.8 us; the launch traced here: 51.7 us
  Pallas kernels  51 us (98%)
  between operations  0.64 us (1%)
    pallas_call x1, Pallas kernels, shards(): pl.pallas_call(kernel, out_shape=(jax.ShapeDtypeStruct((MEMB, ROWS, COLS)...  49.7 us
    pallas_call x1, Pallas kernels, shards(): pl.pallas_call(hand_out, out_shape=[jax.ShapeDtypeStruct(r.shape, r.dtype...  1.36 us

profile of v3, /device:TPU:1, one launch (start us, length us, event | category | flops | bytes accessed | tf_op | source)
XLA Modules:
  0.0 51.7 jit_solution(6911238768717722760)
XLA Ops:
  0.6 49.7 %shard_map.139 = (f32[2,16,16384]{2,1,0:T(8,128)S(1)}, f32[2,40]{1,0:T(2,128)S(1)}, f32[1,40]{1,0:T(1,128)S(1)}) custom-call(f32[2,16,16384]{2,1,0:T(8,128)} %depth.1, f32[16,16384]{1,0:T(8,128)} %bed_in.1, f32[2,16,16384]{2,1,0:T(8,128)} %rain_in.1, s32[16,16384]{1,0:T(8,128)} %rough.1, f32[1,16]{1,0:T(1,128)} %bitcast.9, s32[1,8,32]{2,1,0:T(8,128)} %bitcast.7, ...), custom_call_target="tpu_custom_call" | custom-call | tf_op jit(solution)/shard_map/pallas_call | solution.py:531
  50.3 1.4 %shard_map.140 = (f32[2,16,16384]{2,1,0:T(8,128)}, f32[2,40]{1,0:T(2,128)}, f32[1,40]{1,0:T(1,128)}) custom-call(f32[2,16,16384]{2,1,0:T(8,128)S(1)} %get-tuple-element.9.water, f32[2,40]{1,0:T(2,128)S(1)} %get-tuple-element.10.pool, f32[1,40]{1,0:T(1,128)S(1)} %get-tuple-element.11.outflow), custom_call_target="tpu_custom_call" | custom-call | tf_op jit(solution)/shard_map/pallas_call | solution.py:606

commit v4 on v3

--- a/solution.py
+++ b/solution.py
@@ -51,6 +51,16 @@
 
 def power(water):
     return water * jnp.exp2(jnp.log2(jnp.abs(water)) * (2.0 / 3.0))
+
+
+def merge4(leaves, index, bit):
+    low, high = (index & bit) != 0, (index & (2 * bit)) != 0
+    terms = []
+    for t in range(4):
+        a, b, c, d = [leaves[(q + t) % 4] for q in range(4)]
+        value = jnp.where(high, jnp.where(low, d, c), jnp.where(low, b, a))
+        terms.append(pltpu.roll(value, t * bit, 1) if t else value)
+    return total_of(terms)
 
 
 def peer_offsets():
@@ -301,7 +311,7 @@
 
         turned = tuple(set_levels(0, found))
         for p in range(PARTS):
-            turned = lax.fori_loop(p * SPAN, p * SPAN + SPAN, block, turned, unroll=2)
+            turned = lax.fori_loop(p * SPAN, p * SPAN + SPAN, block, turned, unroll=4)
             if step < STEPS - 1:
                 for copy in halo_copies(step + 1, p):
                     copy.start()
@@ -316,10 +326,8 @@
                         for n in range(0, len(leaves), 2)
                     ]
                 groups.append(leaves[0])
-            for bit in (8, 16, 32, 64):
-                groups = [
-                    merge(groups[n], groups[n + 1], lane, bit, 1) for n in range(0, len(groups), 2)
-                ]
+            for bit in (8, 32):
+                groups = [merge4(groups[n:n + 4], lane, bit) for n in range(0, len(groups), 4)]
             sums.append(groups[0])
         return sums
 
@@ -354,11 +362,7 @@
                 total_of([jnp.where(at == float(p), v, 0.0) for at, v in zip(places, values)])
                 for p in range(4 * j, 4 * j + 4)
             ]
-            for bit in (32, 64):
-                leaves = [
-                    merge(leaves[n], leaves[n + 1], lane, bit, 1) for n in range(0, len(leaves), 2)
-                ]
-            lines[m, j * 8:j * 8 + 8, :] = leaves[0]
+            lines[m, j * 8:j * 8 + 8, :] = merge4(leaves, lane, 32)
 
     def cascade(held, m, v):
         lateral = total_of([lines[m, pl.ds(v * 64 + r, 8, stride=8), :] for r in range(8)])
@@ -415,8 +419,6 @@
         flows(0, m)
 
     pltpu.make_async_copy(greet, greet, isem).wait()
-    for n in range(TILES // 4):
-        pos[n] = jnp.concatenate([greet[4 * n + d, 0:2, :] for d in range(4)], axis=0)
     for k in range(4):
         pick = (lane & 15) * 4 + k
         for b in range(4):
@@ -426,8 +428,7 @@
                 tile = jnp.where((lane >> 4) == kind, lanes_of(rows, pick), tile)
             turn[k * 32 + b * 8:k * 32 + b * 8 + 8, :] = tile
     turn[...] = jnp.transpose(turn[...])
-    for m in range(MEMB + 1):
-        lines[m, 80:128, :] = jnp.zeros((48, 128), F32)
+    links = []
     for v in range(2):
         used = sub + 8 * v < LAKE_DEV // 4
         rows = [turn[16 * kind + 8 * v:16 * kind + 8 * v + 8, :] for kind in range(5)]
@@ -436,11 +437,18 @@
             outf[m, v] = jnp.zeros((8, 128), F32)
         par[0, v] = 1.0 / jnp.where(used, rows[2], 1.0)
         par[1, v] = rows[3]
-        factor = rows[3] * rows[4]
-        run = rows[4]
-        for k in range(DEPTH - 1):
-            chain[k, v] = run
-            run = run * pltpu.roll(factor, k + 1, 1)
+        links.append(rows[4])
+
+    def settle():
+        for n in range(TILES // 4):
+            pos[n] = jnp.concatenate([greet[4 * n + d, 0:2, :] for d in range(4)], axis=0)
+        for m in range(MEMB + 1):
+            lines[m, 80:128, :] = jnp.zeros((48, 128), F32)
+        for v in range(2):
+            factor, run = par[1, v] * links[v], links[v]
+            for k in range(DEPTH - 1):
+                chain[k, v] = run
+                run = run * pltpu.roll(factor, k + 1, 1)
 
     for copy in still_copies:
         copy.wait_recv()
@@ -450,6 +458,8 @@
             hear(step - 1)
         sums = drain(step)
         tell(step, sums)
+        if step == 0:
+            settle()
         if step == STEPS - 1:
             share_start()
         else:

time: 51.8 us -> 51.1 us (0.986)
  Pallas kernels: 51 us -> 50.3 us
    pallas_call x1, Pallas kernels: 49.7 us -> 48.9 us  [shards(): pl.pallas_call(kernel, out_shape=(jax.ShapeDtypeStruct((MEMB, ROWS, COLS)...]
where the time goes in v4:
time: 51.1 us; the launch traced here: 50.9 us
  Pallas kernels  50.3 us (98%)
  between operations  0.64 us (1%)
    pallas_call x1, Pallas kernels, shards(): pl.pallas_call(kernel, out_shape=(jax.ShapeDtypeStruct((MEMB, ROWS, COLS)...  48.9 us
    pallas_call x1, Pallas kernels, shards(): pl.pallas_call(hand_out, out_shape=[jax.ShapeDtypeStruct(r.shape, r.dtype...  1.36 us

profile of v4, /device:TPU:1, one launch (start us, length us, event | category | flops | bytes accessed | tf_op | source)
XLA Modules:
  0.0 50.9 jit_solution(10922650627350946496)
XLA Ops:
  0.6 48.9 %shard_map.139 = (f32[2,16,16384]{2,1,0:T(8,128)S(1)}, f32[2,40]{1,0:T(2,128)S(1)}, f32[1,40]{1,0:T(1,128)S(1)}) custom-call(f32[2,16,16384]{2,1,0:T(8,128)} %depth.1, f32[16,16384]{1,0:T(8,128)} %bed_in.1, f32[2,16,16384]{2,1,0:T(8,128)} %rain_in.1, s32[16,16384]{1,0:T(8,128)} %rough.1, f32[1,16]{1,0:T(1,128)} %bitcast.9, s32[1,8,32]{2,1,0:T(8,128)} %bitcast.7, ...), custom_call_target="tpu_custom_call" | custom-call | tf_op jit(solution)/shard_map/pallas_call | solution.py:541
  49.6 1.4 %shard_map.140 = (f32[2,16,16384]{2,1,0:T(8,128)}, f32[2,40]{1,0:T(2,128)}, f32[1,40]{1,0:T(1,128)}) custom-call(f32[2,16,16384]{2,1,0:T(8,128)S(1)} %get-tuple-element.9.water, f32[2,40]{1,0:T(2,128)S(1)} %get-tuple-element.10.pool, f32[1,40]{1,0:T(1,128)S(1)} %get-tuple-element.11.outflow), custom_call_target="tpu_custom_call" | custom-call | tf_op jit(solution)/shard_map/pallas_call | solution.py:616
